TPU v7x, 128 devices: a whole 4x4x4 slice. The times are simulated.
128 devices in a mesh: pipe: 8 (over y_lo, x), ctx: 16 (over y_hi, z, core).
Axes of the slice: x: 4, y: 4 (y_hi: 2, y_lo: 2; y = y_hi * 2 + y_lo), z: 4, core: 2. Of those that a mesh axis runs over, the one named last changes fastest.
Arguments:
- queries: bfloat16 [8, 8192, 1024], P('pipe', 'ctx'), may hold values from -14 to 14
- keys: bfloat16 [8, 8192, 128], P('pipe', 'ctx'), may hold values from -14 to 14
- values: bfloat16 [8, 8192, 128], P('pipe', 'ctx'), may hold values from -6 to 6
- out_grad: bfloat16 [8, 8192, 1024], P('pipe', 'ctx'), may hold values from -6 to 6
- doc_lengths: int32 [8, 8], P('pipe'), may hold values from 1 to 4096, 8192 in all within a row
- assignment: int32 [8, 16], P('pipe'), may hold values from 0 to 15, each once within a row
Outputs:
- q_grad_in: bfloat16 [8, 8192, 1024], P('pipe', 'ctx')
- k_grad_in: bfloat16 [8, 8192, 128], P('pipe', 'ctx')
- v_grad_in: bfloat16 [8, 8192, 128], P('pipe', 'ctx')
Inputs may be any that keep to these rules, and one draw needn't show every extreme that they name: Each row is a permutation; device i of ctx holds the blocks assignment[s, i] and 31 - assignment[s, i] of 256 positions, in that order. `doc_lengths`: each row sums to 8192 and its largest entry is 4096.
All inputs are finite; a program needn't handle non-finite values.
Results may differ from a plain program's by a relative error of at most 0.0069.
Values may be sent and summed in bfloat16 or wider, within the bound.
No kernel may reach another device: no remote copies, remote signals or barrier semaphores. Data moves between devices by JAX's collectives and lax.ppermute only.
A program may use at most 128 MiB of HBM per device.

v0:
```python
import functools
import math

import jax
import jax.numpy as jnp
from jax import lax
from jax.experimental import pallas as pl
from jax.experimental.pallas import tpu as pltpu
from jax.sharding import PartitionSpec as P


BLK = 256
HD = 128
WINDOW = 17
N_Z = 4
CHUNKS = 2
FAR = 262144.0
EXP_SCALE = math.log2(math.e) / math.sqrt(HD)
SCALE = 1.0 / math.sqrt(HD)


def attention_kernel(
    docs, placing, where, *refs, blocks, heads, chips
):
    q_own, q_par, g_own, g_par = refs[:4]
    pieces = refs[4 : 4 + 2 * chips]
    refs = refs[4 + 2 * chips :]
    own_outs, par_outs, dq_own, dq_par = refs[:chips], refs[chips : chips + 2], *refs[chips + 2 : chips + 4]
    (kv, key_mask, kt, dk, dv, q, g, dq, dqt, even, odd, sem, osem) = refs[chips + 4 :]
    nblk = kv.shape[0]
    half = blocks // 2
    items = blocks * heads
    me = where[0]
    core = lax.rem(me, 2)

    def chip_at(sign, r, swap):
        dy, dz = r // N_Z, r % N_Z
        y = lax.rem(me // (2 * N_Z) + dy, chips // N_Z)
        z = lax.rem(lax.rem(me // 2, N_Z) + sign * dz + N_Z, N_Z)
        return placing[y * 2 * N_Z + z * 2 + (1 - core if swap else core)]

    copies = []
    for i in range(2 * chips):
        at = chip_at(-1, i % chips, i >= chips)
        copies.append(pltpu.make_async_copy(pieces[i].at[pl.ds(0, BLK)], kv.at[at], sem.at[0]))
        copies.append(
            pltpu.make_async_copy(pieces[i].at[pl.ds(BLK, BLK)], kv.at[nblk - 1 - at], sem.at[0])
        )
    for local, (q_src, g_src) in enumerate(((q_own, g_own), (q_par, g_par))):
        for b in range(half):
            for h in range(heads):
                col = pl.multiple_of((core * heads + h) * HD, HD)
                for source, target in ((q_src, q), (g_src, g)):
                    copies.append(
                        pltpu.make_async_copy(
                            source.at[pl.ds(b * BLK, BLK), pl.ds(col, HD)],
                            target.at[local * half + b, h],
                            sem.at[0],
                        )
                    )
    for c in copies:
        c.start()

    own, par = placing[me], placing[me + 1 - 2 * core]
    query_blocks = [own, nblk - 1 - own, par, nblk - 1 - par]
    starts, ends = [], []
    at = jnp.int32(0)
    for i in range(docs.shape[0]):
        starts.append(at)
        at = at + docs[i]
        ends.append(at)
    firsts = []
    for b in query_blocks:
        reach = jnp.int32(0)
        for x in starts:
            reach = jnp.where(x <= b * BLK, x, reach)
        firsts.append(reach // BLK)
    lane = lax.broadcasted_iota(jnp.int32, (BLK, HD), 1)
    row = lax.broadcasted_iota(jnp.int32, (BLK, HD), 0)
    lane_start = jnp.full((BLK, HD), nblk * BLK, jnp.int32)
    lane_end = lane_start
    for i in range(docs.shape[0]):
        lane_start = jnp.where(lane == i, starts[i], lane_start)
        lane_end = jnp.where(lane == i, ends[i], lane_end)
    lane_start, lane_end = lane_start - row, lane_end - row

    def inside(b):
        return (lane_start <= b * BLK) & (b * BLK < lane_end)

    def clear(b, carry):
        dk[b] = jnp.zeros(dk.shape[1:], dk.dtype)
        dv[b] = jnp.zeros(dv.shape[1:], dv.dtype)
        key_mask[b] = jnp.where(inside(b), 0.0, 1.0).astype(jnp.bfloat16)
        return carry

    lax.fori_loop(0, nblk, clear, 0)
    for c in copies:
        c.wait()

    def turn(b, carry):
        used = False
        for top, low in zip(query_blocks, firsts):
            used = used | ((b <= top) & (b >= low))

        @pl.when(used)
        def _():
            kt[b] = kv[b, :, :HD].T

        return carry

    lax.fori_loop(0, nblk, turn, 0)

    def choose(n, options):
        out = options[-1]
        for i in range(len(options) - 1):
            out = jnp.where(n == i, options[i], out)
        return out

    def span(i):
        n = i // heads
        b, lo = choose(n, query_blocks), choose(n, firsts)
        return b, lo, b - lo

    def prepare(i, b, bufs):
        qa, gt = bufs[:2]
        n, h = i // heads, lax.rem(i, heads)
        qa[:HD] = q[n, h].T
        qa[HD:] = jnp.where(inside(b), -FAR, 0.0).astype(jnp.bfloat16).T
        gt[...] = g[n, h].T

    def stats(tile, slot, bufs, state, causal, size):
        qa, gt, ebuf, dbuf, mbuf = bufs
        m, l, d = state
        rows = size * BLK
        kvs = kv[pl.ds(tile, size)].reshape(rows, 2 * HD)
        lhs = jnp.concatenate([kvs[:, :HD], key_mask[pl.ds(tile, size)].reshape(rows, HD)], axis=1)
        s = jnp.dot(lhs, qa[...], preferred_element_type=jnp.float32)
        if causal:
            key_at = lax.broadcasted_iota(jnp.int32, s.shape, 0)
            query_at = lax.broadcasted_iota(jnp.int32, s.shape, 1)
            s = jnp.where(key_at <= query_at, s, -FAR)
        dp = jnp.dot(kvs[:, HD:], gt[...], preferred_element_type=jnp.float32)
        step = BLK // 8 // CHUNKS
        s = s.reshape(size * CHUNKS, step, 8, BLK)
        dp = dp.reshape(size * CHUNKS, step, 8, BLK)
        for c in range(size * CHUNKS):
            at, part = slot + c // CHUNKS, pl.ds(c % CHUNKS * step, step)
            sc, dpc = s[c], dp[c]
            top = jnp.maximum(m, jnp.max(sc, axis=0))
            e = jnp.exp2((sc - top[None]) * EXP_SCALE)
            shrink = jnp.exp2((m - top) * EXP_SCALE)
            ebuf[at, part] = e
            dbuf[at, part] = dpc
            mbuf[at, c % CHUNKS] = top
            m, l, d = (
                top,
                l * shrink + jnp.sum(e, axis=0),
                d * shrink + jnp.sum(e * dpc, axis=0),
            )
        return (m, l, d)

    def grads(tile, slot, bufs, n, h, final, size):
        _, _, ebuf, dbuf, mbuf = bufs
        top, inverse, delta = final
        step = BLK // 8 // CHUNKS
        probs, scores = [], []
        for c in range(size * CHUNKS):
            at, part = slot + c // CHUNKS, pl.ds(c % CHUNKS * step, step)
            fix = jnp.exp2((mbuf[at, c % CHUNKS] - top) * EXP_SCALE) * inverse
            p = ebuf[at, part] * fix[None]
            ds = p * (dbuf[at, part] - delta[None])
            probs.append(p.reshape(BLK // CHUNKS, BLK).astype(jnp.bfloat16))
            scores.append(ds.reshape(BLK // CHUNKS, BLK).astype(jnp.bfloat16))
        p = jnp.concatenate(probs, axis=0)
        ds = jnp.concatenate(scores, axis=0)
        keys_t = jnp.concatenate([kt[tile + i] for i in range(size)], axis=1)
        dqt[...] += jnp.dot(keys_t, ds, preferred_element_type=jnp.float32)
        shape = (size, BLK, HD)
        dv[pl.ds(tile, size)] += jnp.dot(
            p, g[n, h], preferred_element_type=jnp.float32
        ).reshape(shape)
        dk[pl.ds(tile, size)] += jnp.dot(
            ds, q[n, h], preferred_element_type=jnp.float32
        ).reshape(shape)

    def finish(state):
        m, l, d = state
        top = jnp.max(m, axis=0, keepdims=True)
        shrink = jnp.exp2((m - top) * EXP_SCALE)
        inverse = 1.0 / jnp.sum(l * shrink, axis=0, keepdims=True)
        delta = jnp.sum(d * shrink, axis=0, keepdims=True) * inverse
        return (top, inverse, delta)

    none = jnp.full((8, BLK), -FAR, jnp.float32)
    zero = jnp.zeros((8, BLK), jnp.float32)
    fresh = (none, zero, zero)

    def sweep(low, high, body, state):
        pairs = (high - low) // 2
        state = lax.fori_loop(0, pairs, lambda t, st: body(low + 2 * t, 2, st), state)
        return lax.fori_loop(low + 2 * pairs, high, lambda t, st: body(t, 1, st), state)

    def start():
        b, lo, count = span(0)
        prepare(0, b, even)
        state = stats(b, count, even, fresh, True, 1)

        def only(t, size, state):
            return stats(lo + t, t, even, state, False, size)

        return finish(sweep(0, count, only, state))

    def step(i, final, now, later):
        n, h = i // heads, lax.rem(i, heads)
        nxt = jnp.minimum(i + 1, items - 1)
        b, lo, count = span(i)
        b_n, lo_n, count_n = span(nxt)
        todo = jnp.where(i + 1 < items, count_n, 0)
        both = jnp.minimum(count, todo) // 2
        prepare(nxt, b_n, later)
        dqt[...] = jnp.zeros_like(dqt)
        state = stats(b_n, count_n, later, fresh, True, 1)
        grads(b, count, now, n, h, final, 1)

        def joint(t, state):
            state = stats(lo_n + 2 * t, 2 * t, later, state, False, 2)
            grads(lo + 2 * t, 2 * t, now, n, h, final, 2)
            return state

        def ahead(t, size, state):
            return stats(lo_n + t, t, later, state, False, size)

        def behind(t, size, carry):
            grads(lo + t, t, now, n, h, final, size)
            return carry

        state = lax.fori_loop(0, both, joint, state)
        state = sweep(2 * both, todo, ahead, state)
        sweep(2 * both, count, behind, 0)
        dq[n, h] = (dqt[...] * SCALE).T.astype(jnp.bfloat16)
        return finish(state)

    def pair(j, final):
        final = step(2 * j, final, even, odd)
        return step(2 * j + 1, final, odd, even)

    lax.fori_loop(0, items // 2, pair, start())

    back = []
    for local, target in enumerate((dq_own, dq_par)):
        for b in range(half):
            for h in range(heads):
                back.append(
                    pltpu.make_async_copy(
                        dq.at[local * half + b, h],
                        target.at[pl.ds(b * BLK, BLK), pl.ds(h * HD, HD)],
                        osem.at[0],
                    )
                )
    for c in back:
        c.start()
    for i in range(2 * chips):
        at = chip_at(1, i % chips, i >= chips)
        out = own_outs[i] if i < chips else par_outs[(i - chips) // N_Z].at[i % N_Z]
        for first_row, block in ((0, at), (BLK, nblk - 1 - at)):
            out[pl.ds(first_row, BLK), :HD] = (dk[block] * SCALE).astype(jnp.bfloat16)
            out[pl.ds(first_row, BLK), HD:] = dv[block].astype(jnp.bfloat16)
    for c in back:
        c.wait()


def run_attention(docs, placing, where, q_own, q_par, g_own, g_par, pieces):
    chips = len(pieces) // 2
    heads = q_own.shape[1] // HD // 2
    rows = q_own.shape[0]
    blocks, nblk = 2 * rows // BLK, 4 * chips
    hbm = pl.BlockSpec(memory_space=pltpu.HBM)
    vmem = pl.BlockSpec(memory_space=pltpu.VMEM)
    smem = pl.BlockSpec(memory_space=pltpu.SMEM)
    bf16, f32 = jnp.bfloat16, jnp.float32
    part = jax.ShapeDtypeStruct((rows, 2 * HD), bf16)
    parts = jax.ShapeDtypeStruct((N_Z, rows, 2 * HD), bf16)
    grad = jax.ShapeDtypeStruct((rows, heads * HD), bf16)
    work = (
        pltpu.VMEM((2 * HD, BLK), bf16),
        pltpu.VMEM((HD, BLK), bf16),
        pltpu.VMEM((WINDOW, BLK // 8, 8, BLK), f32),
        pltpu.VMEM((WINDOW, BLK // 8, 8, BLK), f32),
        pltpu.VMEM((WINDOW, CHUNKS, 8, BLK), f32),
    )
    return pl.pallas_call(
        functools.partial(attention_kernel, blocks=blocks, heads=heads, chips=chips),
        out_shape=[part] * chips + [parts] * (chips // N_Z) + [grad] * 2,
        in_specs=[smem] * 3 + [hbm] * (4 + 2 * chips),
        out_specs=[vmem] * (chips + chips // N_Z) + [hbm] * 2,
        scratch_shapes=[
            pltpu.VMEM((nblk, BLK, 2 * HD), bf16),
            pltpu.VMEM((nblk, BLK, HD), bf16),
            pltpu.VMEM((nblk, HD, BLK), bf16),
            pltpu.VMEM((nblk, BLK, HD), f32),
            pltpu.VMEM((nblk, BLK, HD), f32),
            pltpu.VMEM((blocks, heads, BLK, HD), bf16),
            pltpu.VMEM((blocks, heads, BLK, HD), bf16),
            pltpu.VMEM((blocks, heads, BLK, HD), bf16),
            pltpu.VMEM((HD, BLK), f32),
            work,
            work,
            pltpu.SemaphoreType.DMA((1,)),
            pltpu.SemaphoreType.DMA((1,)),
        ],
        compiler_params=pltpu.CompilerParams(vmem_limit_bytes=58 * 1024 * 1024),
        name="attention",
    )(docs, placing, where, q_own, q_par, g_own, g_par, *pieces)


def local(queries, keys, values, out_grad, doc_lengths, assignment):
    n_ctx = lax.axis_size("ctx")
    n_pipe = lax.axis_size("pipe")
    me = lax.axis_index("ctx")
    core = me % 2
    n_y = n_ctx // 2 // N_Z

    def hop(x, dy, dz):
        def to(i):
            y, z, c = i // (2 * N_Z), i // 2 % N_Z, i % 2
            return ((y + dy) % n_y) * 2 * N_Z + ((z + dz) % N_Z) * 2 + c

        return lax.ppermute(x, "ctx", [(i, to(i)) for i in range(n_ctx)])

    def swap(x):
        return lax.ppermute(x, "ctx", [(i, i ^ 1) for i in range(n_ctx)])

    q, g = queries[0], out_grad[0]
    packed = jnp.concatenate([keys[0], values[0]], axis=1)
    facing = hop(packed, 1, 0)
    near_in = [hop(packed, 0, dz) for dz in (1, 2, 3)]
    far_in = [hop(facing, 0, 1), hop(near_in[1], 1, 0), hop(facing, 0, 3)]
    mine = [packed] + near_in + [facing] + far_in
    q_par, g_par = swap(q), swap(g)
    others = [swap(x) for x in mine]

    results = run_attention(
        doc_lengths[0].astype(jnp.int32),
        assignment[0].astype(jnp.int32),
        me[None].astype(jnp.int32),
        q,
        q_par,
        g,
        g_par,
        mine + others,
    )
    chips = len(mine)
    own_parts, par_parts = results[:chips], results[chips : chips + n_y]
    dq_own, dq_par = results[chips + n_y :]

    def route(flip):
        pairs = []
        for s in range(n_pipe):
            for i in range(n_ctx):
                to = (s - 1) % n_pipe * n_ctx + (i ^ 1 if flip else i)
                pairs.append((s * n_ctx + i, to))
        return pairs

    def total(parts):
        return functools.reduce(lambda a, b: a + b, [x.astype(jnp.float32) for x in parts])

    far_swap, near_swap = swap(par_parts[1]), swap(par_parts[0])
    dq_same = lax.ppermute(dq_own, ("pipe", "ctx"), route(False))
    dq_flip = lax.ppermute(dq_par, ("pipe", "ctx"), route(True))
    far = [total([own_parts[N_Z + i], far_swap[i]]).astype(jnp.bfloat16) for i in range(N_Z)]
    far2 = hop(far[2], 1, 0)
    far1, far3 = hop(far[1], 0, 1), hop(far[3], 0, 3)
    near = [total([own_parts[i], near_swap[i]]).astype(jnp.bfloat16) for i in (0, 1, 3)]
    near1, near3 = hop(near[1], 0, 1), hop(near[2], 0, 3)
    middle = total([own_parts[2], near_swap[2], far2]).astype(jnp.bfloat16)
    near2 = hop(middle, 0, 2)
    crossed = hop(total([far[0], far1, far3]).astype(jnp.bfloat16), 1, 0)
    kv_grad = total([near[0], near1, near2, near3, crossed])
    kv_out = lax.ppermute(
        kv_grad.astype(jnp.bfloat16), "pipe", [((i + 1) % n_pipe, i) for i in range(n_pipe)]
    )
    left = jnp.where(core == 0, dq_same, dq_flip)
    right = jnp.where(core == 0, dq_flip, dq_same)
    q_out = jnp.concatenate([left, right], axis=1)
    return (q_out[None], kv_out[:, :HD][None], kv_out[:, HD:][None])


def solution(mesh):
    return step_of(mesh, local)


def step_of(mesh, body):
    return jax.shard_map(
        body,
        mesh=mesh,
        in_specs=(
            P("pipe", "ctx", None),
            P("pipe", "ctx", None),
            P("pipe", "ctx", None),
            P("pipe", "ctx", None),
            P("pipe", None),
            P("pipe", None),
        ),
        out_specs=(P("pipe", "ctx", None), P("pipe", "ctx", None), P("pipe", "ctx", None)),
        check_vma=False,
    )
```

profile of v0, /device:TPU:38, one launch (start us, length us, event | category | flops | bytes accessed | tf_op | source)
XLA Modules:
  0.0 152.4 jit_solution(17511204435898853445)
XLA Ops:
  0.6 1.0 pad_maximum_fusion.refs_4_
  1.6 3.3 %collective-permute-start.5 = (bf16[512,256]{1,0:T(8,128)(2,1)S(1)}, bf16[512,256]{1,0:T(8,128)(2,1)S(1)}, u32[]{:S(2)}, u32[]{:S(2)}) collective-permute-start(bf16[512,256]{1,0:T(8,128)(2,1)S(1)} %pad_maximum_fusion.refs_4_), channel_id=1, source_target_pairs={{0,8},{1,9},{2,10},{3,11},{4,12},{5,13},{6,14},{7,15},{8,0},{9,1},... | collective-permute-start | bytes 786440 | tf_op jit(solution)/shard_map/ppermute | solution.py:328
  4.9 3.0 %collective-permute-start.3 = (bf16[512,256]{1,0:T(8,128)(2,1)S(1)}, bf16[512,256]{1,0:T(8,128)(2,1)S(1)}, u32[]{:S(2)}, u32[]{:S(2)}) collective-permute-start(bf16[512,256]{1,0:T(8,128)(2,1)S(1)} %pad_maximum_fusion.refs_4_), channel_id=1, source_target_pairs={{0,4},{1,5},{2,6},{3,7},{4,0},{5,1},{6,2},{7,3},{8,12},{9,13},{10,... | collective-permute-start | bytes 786440 | tf_op jit(solution)/shard_map/ppermute | solution.py:328
  7.9 2.0 %collective-permute-start.4 = (bf16[512,256]{1,0:T(8,128)(2,1)S(1)}, bf16[512,256]{1,0:T(8,128)(2,1)S(1)}, u32[]{:S(2)}, u32[]{:S(2)}) collective-permute-start(bf16[512,256]{1,0:T(8,128)(2,1)S(1)} %pad_maximum_fusion.refs_4_), channel_id=1, source_target_pairs={{0,6},{1,7},{2,0},{3,1},{4,2},{5,3},{6,4},{7,5},{8,14},{9,15},{10,... | collective-permute-start | bytes 786440 | tf_op jit(solution)/shard_map/ppermute | solution.py:328
  9.9 1.3 collective-permute-done.5.refs_8_
  11.3 1.9 %collective-permute-start.6 = (bf16[512,256]{1,0:T(8,128)(2,1)S(1)}, bf16[512,256]{1,0:T(8,128)(2,1)}, u32[]{:S(2)}, u32[]{:S(2)}) collective-permute-start(bf16[512,256]{1,0:T(8,128)(2,1)S(1)} %collective-permute-done.5.refs_8_), channel_id=1, source_target_pairs={{0,2},{1,3},{2,4},{3,5},{4,6},{5,7},{6,0},{7,1},{8,10},{9,11},{10,... | collective-permute-start | bytes 786440 | tf_op jit(solution)/shard_map/ppermute | solution.py:328
  13.2 2.4 %collective-permute-done.3.refs_6_ = bf16[512,256]{1,0:T(8,128)(2,1)S(1)} collective-permute-done((bf16[512,256]{1,0:T(8,128)(2,1)S(1)}, bf16[512,256]{1,0:T(8,128)(2,1)S(1)}, u32[]{:S(2)}, u32[]{:S(2)}) %collective-permute-start.3) | collective-permute-done | bytes 262176 | tf_op jit(solution)/shard_map/ppermute | solution.py:328
  15.6 6.0 %collective-permute-done.2.refs_5_ = bf16[512,256]{1,0:T(8,128)(2,1)S(1)} collective-permute-done((bf16[512,256]{1,0:T(8,128)(2,1)S(1)}, bf16[512,256]{1,0:T(8,128)(2,1)S(1)}, u32[]{:S(2)}, u32[]{:S(2)}) %collective-permute-start.2) | collective-permute-done | bytes 262176 | tf_op jit(solution)/shard_map/ppermute | solution.py:328
  22.2 3.8 %collective-permute-done.6.refs_9_ = bf16[512,256]{1,0:T(8,128)(2,1)} collective-permute-done((bf16[512,256]{1,0:T(8,128)(2,1)S(1)}, bf16[512,256]{1,0:T(8,128)(2,1)}, u32[]{:S(2)}, u32[]{:S(2)}) %collective-permute-start.6) | collective-permute-done | bytes 262176 | tf_op jit(solution)/shard_map/ppermute | solution.py:328
  26.0 4.5 %collective-permute-done.8.refs_11_ = bf16[512,256]{1,0:T(8,128)(2,1)} collective-permute-done((bf16[512,256]{1,0:T(8,128)(2,1)S(1)}, bf16[512,256]{1,0:T(8,128)(2,1)}, u32[]{:S(2)}, u32[]{:S(2)}) %collective-permute-start.8) | collective-permute-done | bytes 262176 | tf_op jit(solution)/shard_map/ppermute | solution.py:328
  30.5 1.6 %collective-permute-done.7.refs_10_ = bf16[512,256]{1,0:T(8,128)(2,1)} collective-permute-done((bf16[512,256]{1,0:T(8,128)(2,1)S(1)}, bf16[512,256]{1,0:T(8,128)(2,1)}, u32[]{:S(2)}, u32[]{:S(2)}) %collective-permute-start.7) | collective-permute-done | bytes 262176 | tf_op jit(solution)/shard_map/ppermute | solution.py:328
  32.1 0.5 collective-permute-start.12
  32.7 0.9 collective-permute-done.10.refs_13_
  34.8 0.8 collective-permute-done.16.refs_19_
  36.0 0.9 copy-done
  37.3 38.6 %attention.1 = (bf16[512,256]{1,0:T(8,128)(2,1)}, bf16[512,256]{1,0:T(8,128)(2,1)}, bf16[512,256]{1,0:T(8,128)(2,1)}, bf16[512,256]{1,0:T(8,128)(2,1)}, bf16[512...) custom-call(s32[8]{0:T(128)} %bitcast.59, ...), custom_call_target="tpu_custom_call" | custom-call | tf_op jit(solution)/shard_map/attention/pallas_call | solution.py:291
  75.9 0.5 collective-permute-start.19
  76.4 2.4 %collective-permute-done.21 = bf16[4,512,256]{2,1,0:T(8,128)(2,1)S(1)} collective-permute-done((bf16[4,512,256]{2,1,0:T(8,128)(2,1)}, bf16[4,512,256]{2,1,0:T(8,128)(2,1)S(1)}, u32[]{:S(2)}, u32[]{:S(2)}) %collective-permute-start.21) | collective-permute-done | bytes 1048608 | tf_op jit(solution)/shard_map/ppermute | solution.py:331
  78.8 1.4 fusion.4
  80.2 11.1 %collective-permute-start.25 = (bf16[512,256]{1,0:T(8,128)(2,1)S(1)}, bf16[512,256]{1,0:T(8,128)(2,1)S(1)}, u32[]{:S(2)}, u32[]{:S(2)}) collective-permute-start(bf16[512,256]{1,0:T(8,128)(2,1)S(1)} %get-tuple-element.32), channel_id=1, source_target_pairs={{0,2},{1,3},{2,4},{3,5},{4,6},{5,7},{6,0},{7,1},{8,10},{9,11},{10,... | collective-permute-start | bytes 786440 | tf_op jit(solution)/shard_map/ppermute | solution.py:328
  91.4 1.5 collective-permute-start.26
  93.2 8.4 %collective-permute-start.20 = (bf16[512,256]{1,0:T(8,128)(2,1)S(1)}, bf16[512,256]{1,0:T(8,128)(2,1)S(1)}, u32[]{:S(2)}, u32[]{:S(2)}) collective-permute-start(bf16[512,256]{1,0:T(8,128)(2,1)S(1)} %get-tuple-element.27), channel_id=1, source_target_pairs={{0,2},{1,3},{2,4},{3,5},{4,6},{5,7},{6,0},{7,1},{8,10},{9,11},{10,... | collective-permute-start | bytes 786440 | tf_op jit(solution)/shard_map/ppermute | solution.py:328
  101.5 3.5 %collective-permute-start.23 = (bf16[512,256]{1,0:T(8,128)(2,1)S(1)}, bf16[512,256]{1,0:T(8,128)(2,1)S(1)}, u32[]{:S(2)}, u32[]{:S(2)}) collective-permute-start(bf16[512,256]{1,0:T(8,128)(2,1)S(1)} %get-tuple-element.29), channel_id=1, source_target_pairs={{0,4},{1,5},{2,6},{3,7},{4,0},{5,1},{6,2},{7,3},{8,12},{9,13},{10,... | collective-permute-start | bytes 786440 | tf_op jit(solution)/shard_map/ppermute | solution.py:328
  105.0 0.8 add_convert_fusion.1
  106.2 5.0 %collective-permute-start.17 = (bf16[512,512]{1,0:T(8,128)(2,1)}, bf16[512,512]{1,0:T(8,128)(2,1)S(1)}, u32[]{:S(2)}, u32[]{:S(2)}) collective-permute-start(bf16[512,512]{1,0:T(8,128)(2,1)} %get-tuple-element.15), channel_id=1, source_target_pairs={{0,112},{1,113},{2,114},{3,115},{4,116},{5,117},{6,118},{7,119},{8... | collective-permute-start | bytes 1572872 | tf_op jit(solution)/shard_map/ppermute | solution.py:368
  111.2 2.8 %collective-permute-start.18 = (bf16[512,512]{1,0:T(8,128)(2,1)}, bf16[512,512]{1,0:T(8,128)(2,1)S(1)}, u32[]{:S(2)}, u32[]{:S(2)}) collective-permute-start(bf16[512,512]{1,0:T(8,128)(2,1)} %get-tuple-element.16), channel_id=1, source_target_pairs={{0,113},{1,112},{2,115},{3,114},{4,117},{5,116},{6,119},{7,118},{8... | collective-permute-start | bytes 1572872 | tf_op jit(solution)/shard_map/ppermute | solution.py:369
  114.0 2.5 %collective-permute-done.24 = bf16[512,256]{1,0:T(8,128)(2,1)} collective-permute-done((bf16[512,256]{1,0:T(8,128)(2,1)S(1)}, bf16[512,256]{1,0:T(8,128)(2,1)}, u32[]{:S(2)}, u32[]{:S(2)}) %collective-permute-start.24) | collective-permute-done | bytes 262176 | tf_op jit(solution)/shard_map/ppermute | solution.py:328
  116.5 23.6 %collective-permute-done.27 = bf16[512,256]{1,0:T(8,128)(2,1)} collective-permute-done((bf16[512,256]{1,0:T(8,128)(2,1)}, bf16[512,256]{1,0:T(8,128)(2,1)}, u32[]{:S(2)}, u32[]{:S(2)}) %collective-permute-start.27) | collective-permute-done | bytes 262176 | tf_op jit(solution)/shard_map/ppermute | solution.py:328
  140.0 1.2 add_convert_fusion
  141.5 1.1 maximum_bitcast_fusion
  142.6 9.1 %collective-permute-done.28 = bf16[512,256]{1,0:T(8,128)(2,1)S(1)} collective-permute-done((bf16[512,256]{1,0:T(8,128)(2,1)S(1)}, bf16[512,256]{1,0:T(8,128)(2,1)S(1)}, u32[]{:S(2)}, u32[]{:S(2)}) %collective-permute-start.28) | collective-permute-done | bytes 262176 | tf_op jit(solution)/shard_map/ppermute | solution.py:379
  151.7 0.7 slice_bitcast_fusion.8
  (69 shorter events, 3.4 us)
Async XLA Ops:
  1.6 34.3 %copy-start.2 = (bf16[512,256]{1,0:T(8,128)(2,1)}, bf16[512,256]{1,0:T(8,128)(2,1)S(1)}, u32[]{:S(2)}) copy-start(bf16[512,256]{1,0:T(8,128)(2,1)S(1)} %pad_maximum_fusion.refs_4_) | copy-start | bytes 786436
  1.6 9.6 %collective-permute-start.5 = (bf16[512,256]{1,0:T(8,128)(2,1)S(1)}, bf16[512,256]{1,0:T(8,128)(2,1)S(1)}, u32[]{:S(2)}, u32[]{:S(2)}) collective-permute-start(bf16[512,256]{1,0:T(8,128)(2,1)S(1)} %pad_maximum_fusion.refs_4_), channel_id=1, source_target_pairs={{0,8},{1,9},{2,10},{3,11},{4,12},{5,13},{6,14},{7,15},{8,0},{9,1},... | collective-permute-start | bytes 786440 | tf_op jit(solution)/shard_map/ppermute | solution.py:328
  4.9 10.7 %collective-permute-start.3 = (bf16[512,256]{1,0:T(8,128)(2,1)S(1)}, bf16[512,256]{1,0:T(8,128)(2,1)S(1)}, u32[]{:S(2)}, u32[]{:S(2)}) collective-permute-start(bf16[512,256]{1,0:T(8,128)(2,1)S(1)} %pad_maximum_fusion.refs_4_), channel_id=1, source_target_pairs={{0,4},{1,5},{2,6},{3,7},{4,0},{5,1},{6,2},{7,3},{8,12},{9,13},{10,... | collective-permute-start | bytes 786440 | tf_op jit(solution)/shard_map/ppermute | solution.py:328
  7.9 13.8 %collective-permute-start.2 = (bf16[512,256]{1,0:T(8,128)(2,1)S(1)}, bf16[512,256]{1,0:T(8,128)(2,1)S(1)}, u32[]{:S(2)}, u32[]{:S(2)}) collective-permute-start(bf16[512,256]{1,0:T(8,128)(2,1)S(1)} %pad_maximum_fusion.refs_4_), channel_id=1, source_target_pairs={{0,2},{1,3},{2,4},{3,5},{4,6},{5,7},{6,0},{7,1},{8,10},{9,11},{10,... | collective-permute-start | bytes 786440 | tf_op jit(solution)/shard_map/ppermute | solution.py:328
  7.9 13.8 %collective-permute-start.4 = (bf16[512,256]{1,0:T(8,128)(2,1)S(1)}, bf16[512,256]{1,0:T(8,128)(2,1)S(1)}, u32[]{:S(2)}, u32[]{:S(2)}) collective-permute-start(bf16[512,256]{1,0:T(8,128)(2,1)S(1)} %pad_maximum_fusion.refs_4_), channel_id=1, source_target_pairs={{0,6},{1,7},{2,0},{3,1},{4,2},{5,3},{6,4},{7,5},{8,14},{9,15},{10,... | collective-permute-start | bytes 786440 | tf_op jit(solution)/shard_map/ppermute | solution.py:328
  9.9 11.9 %collective-permute-start.9 = (bf16[512,256]{1,0:T(8,128)(2,1)S(1)}, bf16[512,256]{1,0:T(8,128)(2,1)S(1)}, u32[]{:S(2)}, u32[]{:S(2)}) collective-permute-start(bf16[512,256]{1,0:T(8,128)(2,1)S(1)} %pad_maximum_fusion.refs_4_), channel_id=1, source_target_pairs={{0,1},{1,0},{2,3},{3,2},{4,5},{5,4},{6,7},{7,6},{8,9},{9,8},{10,11... | collective-permute-start | bytes 786440 | tf_op jit(solution)/shard_map/ppermute | solution.py:331
  11.3 24.7 %copy-start.4 = (bf16[512,256]{1,0:T(8,128)(2,1)}, bf16[512,256]{1,0:T(8,128)(2,1)S(1)}, u32[]{:S(2)}) copy-start(bf16[512,256]{1,0:T(8,128)(2,1)S(1)} %collective-permute-done.5.refs_8_) | copy-start | bytes 786436
  11.3 14.8 %collective-permute-start.6 = (bf16[512,256]{1,0:T(8,128)(2,1)S(1)}, bf16[512,256]{1,0:T(8,128)(2,1)}, u32[]{:S(2)}, u32[]{:S(2)}) collective-permute-start(bf16[512,256]{1,0:T(8,128)(2,1)S(1)} %collective-permute-done.5.refs_8_), channel_id=1, source_target_pairs={{0,2},{1,3},{2,4},{3,5},{4,6},{5,7},{6,0},{7,1},{8,10},{9,11},{10,... | collective-permute-start | bytes 786440 | tf_op jit(solution)/shard_map/ppermute | solution.py:328
  15.6 20.3 %collective-permute-start = (bf16[512,1024]{1,0:T(8,128)(2,1)}, bf16[512,1024]{1,0:T(8,128)(2,1)S(1)}, u32[]{:S(2)}, u32[]{:S(2)}) collective-permute-start(bf16[512,1024]{1,0:T(8,128)(2,1)} %bitcast.53), channel_id=1, source_target_pairs={{0,1},{1,0},{2,3},{3,2},{4,5},{5,4},{6,7},{7,6},{8,9},{9,8},{10,11... | collective-permute-start | bytes 3145736 | tf_op jit(solution)/shard_map/ppermute | solution.py:331
  21.7 14.2 %collective-permute-start.1 = (bf16[512,1024]{1,0:T(8,128)(2,1)}, bf16[512,1024]{1,0:T(8,128)(2,1)S(1)}, u32[]{:S(2)}, u32[]{:S(2)}) collective-permute-start(bf16[512,1024]{1,0:T(8,128)(2,1)} %bitcast.55), channel_id=1, source_target_pairs={{0,1},{1,0},{2,3},{3,2},{4,5},{5,4},{6,7},{7,6},{8,9},{9,8},{10,11... | collective-permute-start | bytes 3145736 | tf_op jit(solution)/shard_map/ppermute | solution.py:331
  21.7 8.8 %collective-permute-start.8 = (bf16[512,256]{1,0:T(8,128)(2,1)S(1)}, bf16[512,256]{1,0:T(8,128)(2,1)}, u32[]{:S(2)}, u32[]{:S(2)}) collective-permute-start(bf16[512,256]{1,0:T(8,128)(2,1)S(1)} %collective-permute-done.5.refs_8_), channel_id=1, source_target_pairs={{0,6},{1,7},{2,0},{3,1},{4,2},{5,3},{6,4},{7,5},{8,14},{9,15},{10,... | collective-permute-start | bytes 786440 | tf_op jit(solution)/shard_map/ppermute | solution.py:328
  21.8 10.3 %collective-permute-start.7 = (bf16[512,256]{1,0:T(8,128)(2,1)S(1)}, bf16[512,256]{1,0:T(8,128)(2,1)}, u32[]{:S(2)}, u32[]{:S(2)}) collective-permute-start(bf16[512,256]{1,0:T(8,128)(2,1)S(1)} %collective-permute-done.3.refs_6_), channel_id=1, source_target_pairs={{0,8},{1,9},{2,10},{3,11},{4,12},{5,13},{6,14},{7,15},{8,0},{9,1},... | collective-permute-start | bytes 786440 | tf_op jit(solution)/shard_map/ppermute | solution.py:328
  26.0 6.1 %collective-permute-start.13 = (bf16[512,256]{1,0:T(8,128)(2,1)S(1)}, bf16[512,256]{1,0:T(8,128)(2,1)S(1)}, u32[]{:S(2)}, u32[]{:S(2)}) collective-permute-start(bf16[512,256]{1,0:T(8,128)(2,1)S(1)} %collective-permute-done.5.refs_8_), channel_id=1, source_target_pairs={{0,1},{1,0},{2,3},{3,2},{4,5},{5,4},{6,7},{7,6},{8,9},{9,8},{10,11... | collective-permute-start | bytes 786440 | tf_op jit(solution)/shard_map/ppermute | solution.py:331
  30.5 2.1 %collective-permute-start.11 = (bf16[512,256]{1,0:T(8,128)(2,1)S(1)}, bf16[512,256]{1,0:T(8,128)(2,1)S(1)}, u32[]{:S(2)}, u32[]{:S(2)}) collective-permute-start(bf16[512,256]{1,0:T(8,128)(2,1)S(1)} %collective-permute-done.3.refs_6_), channel_id=1, source_target_pairs={{0,1},{1,0},{2,3},{3,2},{4,5},{5,4},{6,7},{7,6},{8,9},{9,8},{10,11... | collective-permute-start | bytes 786440 | tf_op jit(solution)/shard_map/ppermute | solution.py:331
  32.1 1.5 %collective-permute-start.10 = (bf16[512,256]{1,0:T(8,128)(2,1)S(1)}, bf16[512,256]{1,0:T(8,128)(2,1)S(1)}, u32[]{:S(2)}, u32[]{:S(2)}) collective-permute-start(bf16[512,256]{1,0:T(8,128)(2,1)S(1)} %collective-permute-done.2.refs_5_), channel_id=1, source_target_pairs={{0,1},{1,0},{2,3},{3,2},{4,5},{5,4},{6,7},{7,6},{8,9},{9,8},{10,11... | collective-permute-start | bytes 786440 | tf_op jit(solution)/shard_map/ppermute | solution.py:331
  32.1 1.9 %collective-permute-start.12 = (bf16[512,256]{1,0:T(8,128)(2,1)S(1)}, bf16[512,256]{1,0:T(8,128)(2,1)S(1)}, u32[]{:S(2)}, u32[]{:S(2)}) collective-permute-start(bf16[512,256]{1,0:T(8,128)(2,1)S(1)} %collective-permute-done.4.refs_7_), channel_id=1, source_target_pairs={{0,1},{1,0},{2,3},{3,2},{4,5},{5,4},{6,7},{7,6},{8,9},{9,8},{10,11... | collective-permute-start | bytes 786440 | tf_op jit(solution)/shard_map/ppermute | solution.py:331
  32.6 2.1 %collective-permute-start.14 = (bf16[512,256]{1,0:T(8,128)(2,1)}, bf16[512,256]{1,0:T(8,128)(2,1)}, u32[]{:S(2)}, u32[]{:S(2)}) collective-permute-start(bf16[512,256]{1,0:T(8,128)(2,1)} %collective-permute-done.6.refs_9_), channel_id=1, source_target_pairs={{0,1},{1,0},{2,3},{3,2},{4,5},{5,4},{6,7},{7,6},{8,9},{9,8},{10,11... | collective-permute-start | bytes 786440 | tf_op jit(solution)/shard_map/ppermute | solution.py:331
  33.7 1.9 %collective-permute-start.16 = (bf16[512,256]{1,0:T(8,128)(2,1)}, bf16[512,256]{1,0:T(8,128)(2,1)}, u32[]{:S(2)}, u32[]{:S(2)}) collective-permute-start(bf16[512,256]{1,0:T(8,128)(2,1)} %collective-permute-done.8.refs_11_), channel_id=1, source_target_pairs={{0,1},{1,0},{2,3},{3,2},{4,5},{5,4},{6,7},{7,6},{8,9},{9,8},{10,11... | collective-permute-start | bytes 786440 | tf_op jit(solution)/shard_map/ppermute | solution.py:331
  34.0 1.9 %collective-permute-start.15 = (bf16[512,256]{1,0:T(8,128)(2,1)}, bf16[512,256]{1,0:T(8,128)(2,1)}, u32[]{:S(2)}, u32[]{:S(2)}) collective-permute-start(bf16[512,256]{1,0:T(8,128)(2,1)} %collective-permute-done.7.refs_10_), channel_id=1, source_target_pairs={{0,1},{1,0},{2,3},{3,2},{4,5},{5,4},{6,7},{7,6},{8,9},{9,8},{10,11... | collective-permute-start | bytes 786440 | tf_op jit(solution)/shard_map/ppermute | solution.py:331
  75.8 3.0 %collective-permute-start.21 = (bf16[4,512,256]{2,1,0:T(8,128)(2,1)}, bf16[4,512,256]{2,1,0:T(8,128)(2,1)S(1)}, u32[]{:S(2)}, u32[]{:S(2)}) collective-permute-start(bf16[4,512,256]{2,1,0:T(8,128)(2,1)} %get-tuple-element.22), channel_id=1, source_target_pairs={{0,1},{1,0},{2,3},{3,2},{4,5},{5,4},{6,7},{7,6},{8,9},{9,8},{10,11... | collective-permute-start | bytes 3145736 | tf_op jit(solution)/shard_map/ppermute | solution.py:331
  75.9 17.0 %collective-permute-start.19 = (bf16[4,512,256]{2,1,0:T(8,128)(2,1)}, bf16[4,512,256]{2,1,0:T(8,128)(2,1)S(1)}, u32[]{:S(2)}, u32[]{:S(2)}) collective-permute-start(bf16[4,512,256]{2,1,0:T(8,128)(2,1)} %get-tuple-element.18), channel_id=1, source_target_pairs={{0,1},{1,0},{2,3},{3,2},{4,5},{5,4},{6,7},{7,6},{8,9},{9,8},{10,11... | collective-permute-start | bytes 3145736 | tf_op jit(solution)/shard_map/ppermute | solution.py:331
  80.1 12.7 %collective-permute-start.22 = (bf16[512,256]{1,0:T(8,128)(2,1)S(1)}, bf16[512,256]{1,0:T(8,128)(2,1)S(1)}, u32[]{:S(2)}, u32[]{:S(2)}) collective-permute-start(bf16[512,256]{1,0:T(8,128)(2,1)S(1)} %get-tuple-element.30), channel_id=1, source_target_pairs={{0,8},{1,9},{2,10},{3,11},{4,12},{5,13},{6,14},{7,15},{8,0},{9,1},... | collective-permute-start | bytes 786440 | tf_op jit(solution)/shard_map/ppermute | solution.py:328
  80.2 24.8 %collective-permute-start.25 = (bf16[512,256]{1,0:T(8,128)(2,1)S(1)}, bf16[512,256]{1,0:T(8,128)(2,1)S(1)}, u32[]{:S(2)}, u32[]{:S(2)}) collective-permute-start(bf16[512,256]{1,0:T(8,128)(2,1)S(1)} %get-tuple-element.32), channel_id=1, source_target_pairs={{0,2},{1,3},{2,4},{3,5},{4,6},{5,7},{6,0},{7,1},{8,10},{9,11},{10,... | collective-permute-start | bytes 786440 | tf_op jit(solution)/shard_map/ppermute | solution.py:328
  91.4 13.6 %collective-permute-start.26 = (bf16[512,256]{1,0:T(8,128)(2,1)S(1)}, bf16[512,256]{1,0:T(8,128)(2,1)S(1)}, u32[]{:S(2)}, u32[]{:S(2)}) collective-permute-start(bf16[512,256]{1,0:T(8,128)(2,1)S(1)} %get-tuple-element.31), channel_id=1, source_target_pairs={{0,6},{1,7},{2,0},{3,1},{4,2},{5,3},{6,4},{7,5},{8,14},{9,15},{10,... | collective-permute-start | bytes 786440 | tf_op jit(solution)/shard_map/ppermute | solution.py:328
  93.2 46.9 %copy-start.3 = (bf16[512,256]{1,0:T(8,128)(2,1)S(1)}, bf16[512,256]{1,0:T(8,128)(2,1)}, u32[]{:S(2)}) copy-start(bf16[512,256]{1,0:T(8,128)(2,1)} %get-tuple-element.17) | copy-start | bytes 786436
  93.2 18.0 %collective-permute-start.20 = (bf16[512,256]{1,0:T(8,128)(2,1)S(1)}, bf16[512,256]{1,0:T(8,128)(2,1)S(1)}, u32[]{:S(2)}, u32[]{:S(2)}) collective-permute-start(bf16[512,256]{1,0:T(8,128)(2,1)S(1)} %get-tuple-element.27), channel_id=1, source_target_pairs={{0,2},{1,3},{2,4},{3,5},{4,6},{5,7},{6,0},{7,1},{8,10},{9,11},{10,... | collective-permute-start | bytes 786440 | tf_op jit(solution)/shard_map/ppermute | solution.py:328
  101.5 12.5 %collective-permute-start.23 = (bf16[512,256]{1,0:T(8,128)(2,1)S(1)}, bf16[512,256]{1,0:T(8,128)(2,1)S(1)}, u32[]{:S(2)}, u32[]{:S(2)}) collective-permute-start(bf16[512,256]{1,0:T(8,128)(2,1)S(1)} %get-tuple-element.29), channel_id=1, source_target_pairs={{0,4},{1,5},{2,6},{3,7},{4,0},{5,1},{6,2},{7,3},{8,12},{9,13},{10,... | collective-permute-start | bytes 786440 | tf_op jit(solution)/shard_map/ppermute | solution.py:328
  105.0 11.4 %collective-permute-start.24 = (bf16[512,256]{1,0:T(8,128)(2,1)S(1)}, bf16[512,256]{1,0:T(8,128)(2,1)}, u32[]{:S(2)}, u32[]{:S(2)}) collective-permute-start(bf16[512,256]{1,0:T(8,128)(2,1)S(1)} %get-tuple-element.28), channel_id=1, source_target_pairs={{0,6},{1,7},{2,0},{3,1},{4,2},{5,3},{6,4},{7,5},{8,14},{9,15},{10,... | collective-permute-start | bytes 786440 | tf_op jit(solution)/shard_map/ppermute | solution.py:328
  105.9 34.2 %collective-permute-start.27 = (bf16[512,256]{1,0:T(8,128)(2,1)}, bf16[512,256]{1,0:T(8,128)(2,1)}, u32[]{:S(2)}, u32[]{:S(2)}) collective-permute-start(bf16[512,256]{1,0:T(8,128)(2,1)} %add_convert_fusion.1), channel_id=1, source_target_pairs={{0,8},{1,9},{2,10},{3,11},{4,12},{5,13},{6,14},{7,15},{8,0},{9,1},... | collective-permute-start | bytes 786440 | tf_op jit(solution)/shard_map/ppermute | solution.py:328
  106.2 35.2 %collective-permute-start.17 = (bf16[512,512]{1,0:T(8,128)(2,1)}, bf16[512,512]{1,0:T(8,128)(2,1)S(1)}, u32[]{:S(2)}, u32[]{:S(2)}) collective-permute-start(bf16[512,512]{1,0:T(8,128)(2,1)} %get-tuple-element.15), channel_id=1, source_target_pairs={{0,112},{1,113},{2,114},{3,115},{4,116},{5,117},{6,118},{7,119},{8... | collective-permute-start | bytes 1572872 | tf_op jit(solution)/shard_map/ppermute | solution.py:368
  111.2 30.2 %collective-permute-start.18 = (bf16[512,512]{1,0:T(8,128)(2,1)}, bf16[512,512]{1,0:T(8,128)(2,1)S(1)}, u32[]{:S(2)}, u32[]{:S(2)}) collective-permute-start(bf16[512,512]{1,0:T(8,128)(2,1)} %get-tuple-element.16), channel_id=1, source_target_pairs={{0,113},{1,112},{2,115},{3,114},{4,117},{5,116},{6,119},{7,118},{8... | collective-permute-start | bytes 1572872 | tf_op jit(solution)/shard_map/ppermute | solution.py:369
  141.3 10.4 %collective-permute-start.28 = (bf16[512,256]{1,0:T(8,128)(2,1)S(1)}, bf16[512,256]{1,0:T(8,128)(2,1)S(1)}, u32[]{:S(2)}, u32[]{:S(2)}) collective-permute-start(bf16[512,256]{1,0:T(8,128)(2,1)S(1)} %add_convert_fusion), channel_id=1, source_target_pairs={{16,0},{32,16},{48,32},{64,48},{80,64},{96,80},{112,96},{0,112},{1... | collective-permute-start | bytes 786440 | tf_op jit(solution)/shard_map/ppermute | solution.py:379
  (14 other events, 123.1 us)
where the time goes:
time: 153 us; the launch traced here: 152 us
  waiting for transfers between devices  59.6 us (39%)
  starting transfers between devices  45 us (29%)
  Pallas kernels  38.6 us (25%)
  other arithmetic  5.82 us (4%)
  local copies, waits for them, and re-layouts  2.54 us (2%)
    ppermute x14, waiting for transfers between devices, hop(): return lax.ppermute(x, 'ctx', [(i, to(i)) for i in range(n_ctx)])  45.8 us
    pallas_call x1, Pallas kernels, run_attention(): pl.pallas_call(functools.partial(attention_kernel, blocks=blocks, heads=h...  38.6 us
    ppermute x14, starting transfers between devices, hop(): return lax.ppermute(x, 'ctx', [(i, to(i)) for i in range(n_ctx)])  35.6 us
    ppermute x1, waiting for transfers between devices, local(): lax.ppermute(kv_grad.astype(jnp.bfloat16), 'pipe', [((i + 1) % n_pipe, i)...  9.12 us
    ppermute x1, starting transfers between devices, local(): dq_same = lax.ppermute(dq_own, ('pipe', 'ctx'), route(False))  5 us
    ppermute x12, waiting for transfers between devices, swap(): return lax.ppermute(x, 'ctx', [(i, i ^ 1) for i in range(n_ctx)])  4.68 us
  transfers between devices with their start and end apart: 29, of which 14 were waited for; matrix products, arithmetic and copies ran while one was open for 3% of the time, Pallas kernels for 0%

commit v1 on v0

--- a/solution.py
+++ b/solution.py
@@ -20,24 +20,26 @@
 
 
 def attention_kernel(
-    docs, placing, where, *refs, blocks, heads, chips
+    table, *refs, blocks, heads, chips
 ):
     q_own, q_par, g_own, g_par = refs[:4]
     pieces = refs[4 : 4 + 2 * chips]
     refs = refs[4 + 2 * chips :]
     own_outs, par_outs, dq_own, dq_par = refs[:chips], refs[chips : chips + 2], *refs[chips + 2 : chips + 4]
-    (kv, key_mask, kt, dk, dv, q, g, dq, dqt, even, odd, sem, osem) = refs[chips + 4 :]
+    (kv, key_mask, kt, dk, dv, q, g, dq, dqt, stage, even, odd, sem, osem) = refs[chips + 4 :]
     nblk = kv.shape[0]
     half = blocks // 2
     items = blocks * heads
-    me = where[0]
+    me = table[0]
+    docs_at = 1 + 2 * chips
+    n_docs = table.shape[0] - docs_at
     core = lax.rem(me, 2)
 
     def chip_at(sign, r, swap):
         dy, dz = r // N_Z, r % N_Z
         y = lax.rem(me // (2 * N_Z) + dy, chips // N_Z)
         z = lax.rem(lax.rem(me // 2, N_Z) + sign * dz + N_Z, N_Z)
-        return placing[y * 2 * N_Z + z * 2 + (1 - core if swap else core)]
+        return table[1 + y * 2 * N_Z + z * 2 + (1 - core if swap else core)]
 
     copies = []
     for i in range(2 * chips):
@@ -46,40 +48,53 @@
         copies.append(
             pltpu.make_async_copy(pieces[i].at[pl.ds(BLK, BLK)], kv.at[nblk - 1 - at], sem.at[0])
         )
-    for local, (q_src, g_src) in enumerate(((q_own, g_own), (q_par, g_par))):
-        for b in range(half):
-            for h in range(heads):
-                col = pl.multiple_of((core * heads + h) * HD, HD)
-                for source, target in ((q_src, q), (g_src, g)):
-                    copies.append(
-                        pltpu.make_async_copy(
-                            source.at[pl.ds(b * BLK, BLK), pl.ds(col, HD)],
-                            target.at[local * half + b, h],
-                            sem.at[0],
-                        )
-                    )
     for c in copies:
         c.start()
 
-    own, par = placing[me], placing[me + 1 - 2 * core]
-    query_blocks = [own, nblk - 1 - own, par, nblk - 1 - par]
+    own, par = table[1 + me], table[2 + me - 2 * core]
     starts, ends = [], []
     at = jnp.int32(0)
-    for i in range(docs.shape[0]):
+    for i in range(n_docs):
         starts.append(at)
-        at = at + docs[i]
+        at = at + table[docs_at + i]
         ends.append(at)
-    firsts = []
-    for b in query_blocks:
+
+    def first_tile(b):
         reach = jnp.int32(0)
         for x in starts:
             reach = jnp.where(x <= b * BLK, x, reach)
-        firsts.append(reach // BLK)
+        return reach // BLK
+
+    query_blocks, firsts, halves = [], [], []
+    for local, x in enumerate((own, par)):
+        y = nblk - 1 - x
+        x_low, y_low = first_tile(x), first_tile(y)
+        less = (x - x_low) < (y - y_low)
+        flip = less == (local == 1)
+        query_blocks += [jnp.where(flip, y, x), jnp.where(flip, x, y)]
+        firsts += [jnp.where(flip, y_low, x_low), jnp.where(flip, x_low, y_low)]
+        second = flip.astype(jnp.int32)
+        halves += [second, 1 - second]
+    more = []
+    for n in range(blocks):
+        q_src, g_src = ((q_own, g_own), (q_par, g_par))[n // half]
+        at_row = pl.multiple_of(halves[n] * BLK, BLK)
+        for h in range(heads):
+            col = pl.multiple_of((core * heads + h) * HD, HD)
+            for source, target in ((q_src, q), (g_src, g)):
+                more.append(
+                    pltpu.make_async_copy(
+                        source.at[pl.ds(at_row, BLK), pl.ds(col, HD)], target.at[n, h], sem.at[0]
+                    )
+                )
+    for c in more:
+        c.start()
+    copies += more
     lane = lax.broadcasted_iota(jnp.int32, (BLK, HD), 1)
     row = lax.broadcasted_iota(jnp.int32, (BLK, HD), 0)
     lane_start = jnp.full((BLK, HD), nblk * BLK, jnp.int32)
     lane_end = lane_start
-    for i in range(docs.shape[0]):
+    for i in range(n_docs):
         lane_start = jnp.where(lane == i, starts[i], lane_start)
         lane_end = jnp.where(lane == i, ends[i], lane_end)
     lane_start, lane_end = lane_start - row, lane_end - row
@@ -247,35 +262,37 @@
     lax.fori_loop(0, items // 2, pair, start())
 
     back = []
-    for local, target in enumerate((dq_own, dq_par)):
-        for b in range(half):
-            for h in range(heads):
-                back.append(
-                    pltpu.make_async_copy(
-                        dq.at[local * half + b, h],
-                        target.at[pl.ds(b * BLK, BLK), pl.ds(h * HD, HD)],
-                        osem.at[0],
-                    )
+    for n in range(blocks):
+        at_row = pl.multiple_of(halves[n] * BLK, BLK)
+        for h in range(heads):
+            back.append(
+                pltpu.make_async_copy(
+                    dq.at[n, h],
+                    (dq_own, dq_par)[n // half].at[pl.ds(at_row, BLK), pl.ds(h * HD, HD)],
+                    osem.at[0],
                 )
+            )
     for c in back:
         c.start()
-    for i in range(2 * chips):
+    for i in list(range(chips + N_Z, 2 * chips)) + list(range(N_Z, chips + N_Z)) + list(range(N_Z)):
         at = chip_at(1, i % chips, i >= chips)
+        for first_row, block in ((0, at), (BLK, nblk - 1 - at)):
+            stage[i, pl.ds(first_row, BLK), :HD] = (dk[block] * SCALE).astype(jnp.bfloat16)
+            stage[i, pl.ds(first_row, BLK), HD:] = dv[block].astype(jnp.bfloat16)
         out = own_outs[i] if i < chips else par_outs[(i - chips) // N_Z].at[i % N_Z]
-        for first_row, block in ((0, at), (BLK, nblk - 1 - at)):
-            out[pl.ds(first_row, BLK), :HD] = (dk[block] * SCALE).astype(jnp.bfloat16)
-            out[pl.ds(first_row, BLK), HD:] = dv[block].astype(jnp.bfloat16)
+        c = pltpu.make_async_copy(stage.at[i], out, osem.at[0])
+        c.start()
+        back.append(c)
     for c in back:
         c.wait()
 
 
-def run_attention(docs, placing, where, q_own, q_par, g_own, g_par, pieces):
+def run_attention(table, q_own, q_par, g_own, g_par, pieces):
     chips = len(pieces) // 2
     heads = q_own.shape[1] // HD // 2
     rows = q_own.shape[0]
     blocks, nblk = 2 * rows // BLK, 4 * chips
-    hbm = pl.BlockSpec(memory_space=pltpu.HBM)
-    vmem = pl.BlockSpec(memory_space=pltpu.VMEM)
+    hbm = pl.BlockSpec(memory_space=pl.ANY)
     smem = pl.BlockSpec(memory_space=pltpu.SMEM)
     bf16, f32 = jnp.bfloat16, jnp.float32
     part = jax.ShapeDtypeStruct((rows, 2 * HD), bf16)
@@ -291,8 +308,8 @@
     return pl.pallas_call(
         functools.partial(attention_kernel, blocks=blocks, heads=heads, chips=chips),
         out_shape=[part] * chips + [parts] * (chips // N_Z) + [grad] * 2,
-        in_specs=[smem] * 3 + [hbm] * (4 + 2 * chips),
-        out_specs=[vmem] * (chips + chips // N_Z) + [hbm] * 2,
+        in_specs=[smem] + [hbm] * (4 + 2 * chips),
+        out_specs=[hbm] * (chips + chips // N_Z + 2),
         scratch_shapes=[
             pltpu.VMEM((nblk, BLK, 2 * HD), bf16),
             pltpu.VMEM((nblk, BLK, HD), bf16),
@@ -303,14 +320,15 @@
             pltpu.VMEM((blocks, heads, BLK, HD), bf16),
             pltpu.VMEM((blocks, heads, BLK, HD), bf16),
             pltpu.VMEM((HD, BLK), f32),
+            pltpu.VMEM((2 * chips, rows, 2 * HD), bf16),
             work,
             work,
             pltpu.SemaphoreType.DMA((1,)),
             pltpu.SemaphoreType.DMA((1,)),
         ],
-        compiler_params=pltpu.CompilerParams(vmem_limit_bytes=58 * 1024 * 1024),
+        compiler_params=pltpu.CompilerParams(vmem_limit_bytes=46 * 1024 * 1024),
         name="attention",
-    )(docs, placing, where, q_own, q_par, g_own, g_par, *pieces)
+    )(table, q_own, q_par, g_own, g_par, *pieces)
 
 
 def local(queries, keys, values, out_grad, doc_lengths, assignment):
@@ -340,9 +358,7 @@
     others = [swap(x) for x in mine]
 
     results = run_attention(
-        doc_lengths[0].astype(jnp.int32),
-        assignment[0].astype(jnp.int32),
-        me[None].astype(jnp.int32),
+        jnp.concatenate([me[None], assignment[0], doc_lengths[0]]).astype(jnp.int32),
         q,
         q_par,
         g,
@@ -368,17 +384,26 @@
     dq_same = lax.ppermute(dq_own, ("pipe", "ctx"), route(False))
     dq_flip = lax.ppermute(dq_par, ("pipe", "ctx"), route(True))
     far = [total([own_parts[N_Z + i], far_swap[i]]).astype(jnp.bfloat16) for i in range(N_Z)]
+    far = lax.optimization_barrier(far)
     far2 = hop(far[2], 1, 0)
     far1, far3 = hop(far[1], 0, 1), hop(far[3], 0, 3)
     near = [total([own_parts[i], near_swap[i]]).astype(jnp.bfloat16) for i in (0, 1, 3)]
-    near1, near3 = hop(near[1], 0, 1), hop(near[2], 0, 3)
+    near0, near1, near3, near_swap = lax.optimization_barrier((*near, near_swap))
+    near1, near3 = hop(near1, 0, 1), hop(near3, 0, 3)
     middle = total([own_parts[2], near_swap[2], far2]).astype(jnp.bfloat16)
     near2 = hop(middle, 0, 2)
-    crossed = hop(total([far[0], far1, far3]).astype(jnp.bfloat16), 1, 0)
-    kv_grad = total([near[0], near1, near2, near3, crossed])
-    kv_out = lax.ppermute(
-        kv_grad.astype(jnp.bfloat16), "pipe", [((i + 1) % n_pipe, i) for i in range(n_pipe)]
-    )
+
+    def across(x, dy):
+        pairs = []
+        for s in range(n_pipe):
+            for i in range(n_ctx):
+                to = (s - 1) % n_pipe * n_ctx + (i + dy * 2 * N_Z) % n_ctx
+                pairs.append((s * n_ctx + i, to))
+        return lax.ppermute(x, ("pipe", "ctx"), pairs)
+
+    crossed = across(total([far[0], far1, far3]).astype(jnp.bfloat16), 1)
+    straight = across(total([near0, near1, near2, near3]).astype(jnp.bfloat16), 0)
+    kv_out = total([crossed, straight]).astype(jnp.bfloat16)
     left = jnp.where(core == 0, dq_same, dq_flip)
     right = jnp.where(core == 0, dq_flip, dq_same)
     q_out = jnp.concatenate([left, right], axis=1)

time: 153 us -> 162 us (1.059)
  the two profiles are of different devices: /device:TPU:38 before, /device:TPU:14 now
where the time goes in v1:
time: 162 us
  waiting for transfers between devices  81.1 us (50%)
  Pallas kernels  42.9 us (26%)
  starting transfers between devices  32 us (20%)
  other arithmetic  4.51 us (3%)
    ppermute x13, waiting for transfers between devices, hop(): return lax.ppermute(x, 'ctx', [(i, to(i)) for i in range(n_ctx)])  64.8 us
    pallas_call x1, Pallas kernels, run_attention(): pl.pallas_call(functools.partial(attention_kernel, blocks=blocks, heads=h...  42.9 us
    ppermute x13, starting transfers between devices, hop(): return lax.ppermute(x, 'ctx', [(i, to(i)) for i in range(n_ctx)])  26.4 us
    ppermute x2, waiting for transfers between devices, across(): return lax.ppermute(x, ('pipe', 'ctx'), pairs)  15.4 us
  transfers between devices with their start and end apart: 29, of which 12 were waited for; matrix products, arithmetic and copies ran while one was open for 2% of the time, Pallas kernels for 0%

profile of v1, /device:TPU:14, one launch (start us, length us, event | category | flops | bytes accessed | tf_op | source)
XLA Modules:
  0.0 161.9 jit_solution(5866211087613369128)
XLA Ops:
  0.6 1.0 pad_maximum_fusion.refs_4_
  1.6 2.4 %collective-permute-start.5 = (bf16[512,256]{1,0:T(8,128)(2,1)S(1)}, bf16[512,256]{1,0:T(8,128)(2,1)S(1)}, u32[]{:S(2)}, u32[]{:S(2)}) collective-permute-start(bf16[512,256]{1,0:T(8,128)(2,1)S(1)} %pad_maximum_fusion.refs_4_), channel_id=1, source_target_pairs={{0,8},{1,9},{2,10},{3,11},{4,12},{5,13},{6,14},{7,15},{8,0},{9,1},... | collective-permute-start | bytes 786440 | tf_op jit(solution)/shard_map/ppermute | solution.py:346
  4.0 4.0 %collective-permute-start.4 = (bf16[512,256]{1,0:T(8,128)(2,1)S(1)}, bf16[512,256]{1,0:T(8,128)(2,1)S(1)}, u32[]{:S(2)}, u32[]{:S(2)}) collective-permute-start(bf16[512,256]{1,0:T(8,128)(2,1)S(1)} %pad_maximum_fusion.refs_4_), channel_id=1, source_target_pairs={{0,6},{1,7},{2,0},{3,1},{4,2},{5,3},{6,4},{7,5},{8,14},{9,15},{10,... | collective-permute-start | bytes 786440 | tf_op jit(solution)/shard_map/ppermute | solution.py:346
  8.1 1.3 collective-permute-start.2
  9.3 2.0 %collective-permute-done.5.refs_8_ = bf16[512,256]{1,0:T(8,128)(2,1)S(1)} collective-permute-done((bf16[512,256]{1,0:T(8,128)(2,1)S(1)}, bf16[512,256]{1,0:T(8,128)(2,1)S(1)}, u32[]{:S(2)}, u32[]{:S(2)}) %collective-permute-start.5) | collective-permute-done | bytes 262176 | tf_op jit(solution)/shard_map/ppermute | solution.py:346
  11.3 0.5 collective-permute-start
  11.8 8.1 %collective-permute-done.4.refs_7_ = bf16[512,256]{1,0:T(8,128)(2,1)S(1)} collective-permute-done((bf16[512,256]{1,0:T(8,128)(2,1)S(1)}, bf16[512,256]{1,0:T(8,128)(2,1)S(1)}, u32[]{:S(2)}, u32[]{:S(2)}) %collective-permute-start.4) | collective-permute-done | bytes 262176 | tf_op jit(solution)/shard_map/ppermute | solution.py:346
  19.9 3.7 %collective-permute-start.8 = (bf16[512,256]{1,0:T(8,128)(2,1)S(1)}, bf16[512,256]{1,0:T(8,128)(2,1)S(1)}, u32[]{:S(2)}, u32[]{:S(2)}) collective-permute-start(bf16[512,256]{1,0:T(8,128)(2,1)S(1)} %collective-permute-done.5.refs_8_), channel_id=1, source_target_pairs={{0,6},{1,7},{2,0},{3,1},{4,2},{5,3},{6,4},{7,5},{8,14},{9,15},{10,... | collective-permute-start | bytes 786440 | tf_op jit(solution)/shard_map/ppermute | solution.py:346
  23.6 0.3 collective-permute-start.12
  23.9 5.9 %collective-permute-done.8.refs_11_ = bf16[512,256]{1,0:T(8,128)(2,1)S(1)} collective-permute-done((bf16[512,256]{1,0:T(8,128)(2,1)S(1)}, bf16[512,256]{1,0:T(8,128)(2,1)S(1)}, u32[]{:S(2)}, u32[]{:S(2)}) %collective-permute-start.8) | collective-permute-done | bytes 262176 | tf_op jit(solution)/shard_map/ppermute | solution.py:346
  29.8 3.4 %collective-permute-done.6.refs_9_ = bf16[512,256]{1,0:T(8,128)(2,1)S(1)} collective-permute-done((bf16[512,256]{1,0:T(8,128)(2,1)S(1)}, bf16[512,256]{1,0:T(8,128)(2,1)S(1)}, u32[]{:S(2)}, u32[]{:S(2)}) %collective-permute-start.6) | collective-permute-done | bytes 262176 | tf_op jit(solution)/shard_map/ppermute | solution.py:346
  33.3 1.2 collective-permute-start.7
  34.5 0.5 collective-permute-start.16
  35.0 7.3 %collective-permute-done.7.refs_10_ = bf16[512,256]{1,0:T(8,128)(2,1)S(1)} collective-permute-done((bf16[512,256]{1,0:T(8,128)(2,1)S(1)}, bf16[512,256]{1,0:T(8,128)(2,1)S(1)}, u32[]{:S(2)}, u32[]{:S(2)}) %collective-permute-start.7) | collective-permute-done | bytes 262176 | tf_op jit(solution)/shard_map/ppermute | solution.py:346
  42.3 0.5 collective-permute-start.15
  42.9 0.7 pad_add_fusion.table
  43.6 0.4 collective-permute-done.14.refs_17_
  44.0 0.4 collective-permute-done.15.refs_18_
  44.4 42.9 %attention.1 = (bf16[512,256]{1,0:T(8,128)(2,1)S(1)}, bf16[512,256]{1,0:T(8,128)(2,1)S(1)}, bf16[512,256]{1,0:T(8,128)(2,1)S(1)}, bf16[512,256]{1,0:T(8,128)(2,1...) custom-call(s32[25]{0:T(128)S(1)} %pad_add_fusion.table, ...), custom_call_target="tpu_custom_call" | custom-call | tf_op jit(solution)/shard_map/attention/pallas_call | solution.py:308
  87.5 0.4 collective-permute-start.23
  87.9 3.0 %collective-permute-start.17 = (bf16[512,512]{1,0:T(8,128)(2,1)}, bf16[512,512]{1,0:T(8,128)(2,1)S(1)}, u32[]{:S(2)}, u32[]{:S(2)}) collective-permute-start(bf16[512,512]{1,0:T(8,128)(2,1)} %get-tuple-element.23), channel_id=1, source_target_pairs={{0,112},{1,113},{2,114},{3,115},{4,116},{5,117},{6,118},{7,119},{8... | collective-permute-start | bytes 1572872 | tf_op jit(solution)/shard_map/ppermute | solution.py:384
  90.9 0.3 fusion.5
  91.2 5.0 %collective-permute-start.20 = (bf16[512,256]{1,0:T(8,128)(2,1)S(1)}, bf16[512,256]{1,0:T(8,128)(2,1)S(1)}, u32[]{:S(2)}, u32[]{:S(2)}) collective-permute-start(bf16[512,256]{1,0:T(8,128)(2,1)S(1)} %get-tuple-element.31), channel_id=1, source_target_pairs={{0,2},{1,3},{2,4},{3,5},{4,6},{5,7},{6,0},{7,1},{8,10},{9,11},{10,... | collective-permute-start | bytes 786440 | tf_op jit(solution)/shard_map/ppermute | solution.py:346
  96.3 5.6 %collective-permute-start.25 = (bf16[512,256]{1,0:T(8,128)(2,1)S(1)}, bf16[512,256]{1,0:T(8,128)(2,1)S(1)}, u32[]{:S(2)}, u32[]{:S(2)}) collective-permute-start(bf16[512,256]{1,0:T(8,128)(2,1)S(1)} %get-tuple-element.41), channel_id=1, source_target_pairs={{0,8},{1,9},{2,10},{3,11},{4,12},{5,13},{6,14},{7,15},{8,0},{9,1},... | collective-permute-start | bytes 786440 | tf_op jit(solution)/shard_map/ppermute | solution.py:346
  102.0 27.1 %collective-permute-done.25 = bf16[512,256]{1,0:T(8,128)(2,1)S(1)} collective-permute-done((bf16[512,256]{1,0:T(8,128)(2,1)S(1)}, bf16[512,256]{1,0:T(8,128)(2,1)S(1)}, u32[]{:S(2)}, u32[]{:S(2)}) %collective-permute-start.25) | collective-permute-done | bytes 262176 | tf_op jit(solution)/shard_map/ppermute | solution.py:346
  129.1 0.8 fusion.1
  129.9 3.2 %collective-permute-start.27 = (bf16[512,256]{1,0:T(8,128)(2,1)S(1)}, bf16[512,256]{1,0:T(8,128)(2,1)S(1)}, u32[]{:S(2)}, u32[]{:S(2)}) collective-permute-start(bf16[512,256]{1,0:T(8,128)(2,1)S(1)} %get-tuple-element.42), channel_id=1, source_target_pairs={{0,6},{1,7},{2,0},{3,1},{4,2},{5,3},{6,4},{7,5},{8,14},{9,15},{10,... | collective-permute-start | bytes 786440 | tf_op jit(solution)/shard_map/ppermute | solution.py:346
  133.3 10.9 %collective-permute-done.24 = bf16[512,256]{1,0:T(8,128)(2,1)S(1)} collective-permute-done((bf16[512,256]{1,0:T(8,128)(2,1)S(1)}, bf16[512,256]{1,0:T(8,128)(2,1)S(1)}, u32[]{:S(2)}, u32[]{:S(2)}) %collective-permute-start.24) | collective-permute-done | bytes 262176 | tf_op jit(solution)/shard_map/ppermute | solution.py:346
  144.6 1.1 maximum_bitcast_fusion
  145.7 9.8 %collective-permute-done.22 = bf16[512,256]{1,0:T(8,128)(2,1)S(1)} collective-permute-done((bf16[512,256]{1,0:T(8,128)(2,1)S(1)}, bf16[512,256]{1,0:T(8,128)(2,1)S(1)}, u32[]{:S(2)}, u32[]{:S(2)}) %collective-permute-start.22) | collective-permute-done | bytes 262176 | tf_op jit(solution)/shard_map/ppermute | solution.py:402
  155.4 5.6 %collective-permute-done.28 = bf16[512,256]{1,0:T(8,128)(2,1)S(1)} collective-permute-done((bf16[512,256]{1,0:T(8,128)(2,1)S(1)}, bf16[512,256]{1,0:T(8,128)(2,1)S(1)}, u32[]{:S(2)}, u32[]{:S(2)}) %collective-permute-start.28) | collective-permute-done | bytes 262176 | tf_op jit(solution)/shard_map/ppermute | solution.py:402
  161.2 0.7 slice_bitcast_fusion.7
  (38 shorter events, 1.0 us)
Async XLA Ops:
  1.6 9.6 %collective-permute-start.5 = (bf16[512,256]{1,0:T(8,128)(2,1)S(1)}, bf16[512,256]{1,0:T(8,128)(2,1)S(1)}, u32[]{:S(2)}, u32[]{:S(2)}) collective-permute-start(bf16[512,256]{1,0:T(8,128)(2,1)S(1)} %pad_maximum_fusion.refs_4_), channel_id=1, source_target_pairs={{0,8},{1,9},{2,10},{3,11},{4,12},{5,13},{6,14},{7,15},{8,0},{9,1},... | collective-permute-start | bytes 786440 | tf_op jit(solution)/shard_map/ppermute | solution.py:346
  4.0 7.3 %collective-permute-start.9 = (bf16[512,256]{1,0:T(8,128)(2,1)S(1)}, bf16[512,256]{1,0:T(8,128)(2,1)S(1)}, u32[]{:S(2)}, u32[]{:S(2)}) collective-permute-start(bf16[512,256]{1,0:T(8,128)(2,1)S(1)} %pad_maximum_fusion.refs_4_), channel_id=1, source_target_pairs={{0,1},{1,0},{2,3},{3,2},{4,5},{5,4},{6,7},{7,6},{8,9},{9,8},{10,11... | collective-permute-start | bytes 786440 | tf_op jit(solution)/shard_map/ppermute | solution.py:349
  4.0 15.9 %collective-permute-start.4 = (bf16[512,256]{1,0:T(8,128)(2,1)S(1)}, bf16[512,256]{1,0:T(8,128)(2,1)S(1)}, u32[]{:S(2)}, u32[]{:S(2)}) collective-permute-start(bf16[512,256]{1,0:T(8,128)(2,1)S(1)} %pad_maximum_fusion.refs_4_), channel_id=1, source_target_pairs={{0,6},{1,7},{2,0},{3,1},{4,2},{5,3},{6,4},{7,5},{8,14},{9,15},{10,... | collective-permute-start | bytes 786440 | tf_op jit(solution)/shard_map/ppermute | solution.py:346
  8.0 11.9 %collective-permute-start.3 = (bf16[512,256]{1,0:T(8,128)(2,1)S(1)}, bf16[512,256]{1,0:T(8,128)(2,1)S(1)}, u32[]{:S(2)}, u32[]{:S(2)}) collective-permute-start(bf16[512,256]{1,0:T(8,128)(2,1)S(1)} %pad_maximum_fusion.refs_4_), channel_id=1, source_target_pairs={{0,4},{1,5},{2,6},{3,7},{4,0},{5,1},{6,2},{7,3},{8,12},{9,13},{10,... | collective-permute-start | bytes 786440 | tf_op jit(solution)/shard_map/ppermute | solution.py:346
  8.1 15.6 %collective-permute-start.2 = (bf16[512,256]{1,0:T(8,128)(2,1)S(1)}, bf16[512,256]{1,0:T(8,128)(2,1)S(1)}, u32[]{:S(2)}, u32[]{:S(2)}) collective-permute-start(bf16[512,256]{1,0:T(8,128)(2,1)S(1)} %pad_maximum_fusion.refs_4_), channel_id=1, source_target_pairs={{0,2},{1,3},{2,4},{3,5},{4,6},{5,7},{6,0},{7,1},{8,10},{9,11},{10,... | collective-permute-start | bytes 786440 | tf_op jit(solution)/shard_map/ppermute | solution.py:346
  11.3 12.4 %collective-permute-start.13 = (bf16[512,256]{1,0:T(8,128)(2,1)S(1)}, bf16[512,256]{1,0:T(8,128)(2,1)S(1)}, u32[]{:S(2)}, u32[]{:S(2)}) collective-permute-start(bf16[512,256]{1,0:T(8,128)(2,1)S(1)} %collective-permute-done.5.refs_8_), channel_id=1, source_target_pairs={{0,1},{1,0},{2,3},{3,2},{4,5},{5,4},{6,7},{7,6},{8,9},{9,8},{10,11... | collective-permute-start | bytes 786440 | tf_op jit(solution)/shard_map/ppermute | solution.py:349
  11.3 33.1 %collective-permute-start = (bf16[512,1024]{1,0:T(8,128)(2,1)}, bf16[512,1024]{1,0:T(8,128)(2,1)}, u32[]{:S(2)}, u32[]{:S(2)}) collective-permute-start(bf16[512,1024]{1,0:T(8,128)(2,1)} %bitcast.51), channel_id=1, source_target_pairs={{0,1},{1,0},{2,3},{3,2},{4,5},{5,4},{6,7},{7,6},{8,9},{9,8},{10,11... | collective-permute-start | bytes 3145736 | tf_op jit(solution)/shard_map/ppermute | solution.py:349
  19.9 24.5 %collective-permute-start.1 = (bf16[512,1024]{1,0:T(8,128)(2,1)}, bf16[512,1024]{1,0:T(8,128)(2,1)}, u32[]{:S(2)}, u32[]{:S(2)}) collective-permute-start(bf16[512,1024]{1,0:T(8,128)(2,1)} %bitcast.53), channel_id=1, source_target_pairs={{0,1},{1,0},{2,3},{3,2},{4,5},{5,4},{6,7},{7,6},{8,9},{9,8},{10,11... | collective-permute-start | bytes 3145736 | tf_op jit(solution)/shard_map/ppermute | solution.py:349
  19.9 9.9 %collective-permute-start.8 = (bf16[512,256]{1,0:T(8,128)(2,1)S(1)}, bf16[512,256]{1,0:T(8,128)(2,1)S(1)}, u32[]{:S(2)}, u32[]{:S(2)}) collective-permute-start(bf16[512,256]{1,0:T(8,128)(2,1)S(1)} %collective-permute-done.5.refs_8_), channel_id=1, source_target_pairs={{0,6},{1,7},{2,0},{3,1},{4,2},{5,3},{6,4},{7,5},{8,14},{9,15},{10,... | collective-permute-start | bytes 786440 | tf_op jit(solution)/shard_map/ppermute | solution.py:346
  23.6 9.6 %collective-permute-start.6 = (bf16[512,256]{1,0:T(8,128)(2,1)S(1)}, bf16[512,256]{1,0:T(8,128)(2,1)S(1)}, u32[]{:S(2)}, u32[]{:S(2)}) collective-permute-start(bf16[512,256]{1,0:T(8,128)(2,1)S(1)} %collective-permute-done.5.refs_8_), channel_id=1, source_target_pairs={{0,2},{1,3},{2,4},{3,5},{4,6},{5,7},{6,0},{7,1},{8,10},{9,11},{10,... | collective-permute-start | bytes 786440 | tf_op jit(solution)/shard_map/ppermute | solution.py:346
  23.6 10.9 %collective-permute-start.12 = (bf16[512,256]{1,0:T(8,128)(2,1)S(1)}, bf16[512,256]{1,0:T(8,128)(2,1)S(1)}, u32[]{:S(2)}, u32[]{:S(2)}) collective-permute-start(bf16[512,256]{1,0:T(8,128)(2,1)S(1)} %collective-permute-done.4.refs_7_), channel_id=1, source_target_pairs={{0,1},{1,0},{2,3},{3,2},{4,5},{5,4},{6,7},{7,6},{8,9},{9,8},{10,11... | collective-permute-start | bytes 786440 | tf_op jit(solution)/shard_map/ppermute | solution.py:349
  29.8 4.7 %collective-permute-start.11 = (bf16[512,256]{1,0:T(8,128)(2,1)S(1)}, bf16[512,256]{1,0:T(8,128)(2,1)S(1)}, u32[]{:S(2)}, u32[]{:S(2)}) collective-permute-start(bf16[512,256]{1,0:T(8,128)(2,1)S(1)} %collective-permute-done.3.refs_6_), channel_id=1, source_target_pairs={{0,1},{1,0},{2,3},{3,2},{4,5},{5,4},{6,7},{7,6},{8,9},{9,8},{10,11... | collective-permute-start | bytes 786440 | tf_op jit(solution)/shard_map/ppermute | solution.py:349
  33.3 9.1 %collective-permute-start.7 = (bf16[512,256]{1,0:T(8,128)(2,1)S(1)}, bf16[512,256]{1,0:T(8,128)(2,1)S(1)}, u32[]{:S(2)}, u32[]{:S(2)}) collective-permute-start(bf16[512,256]{1,0:T(8,128)(2,1)S(1)} %collective-permute-done.3.refs_6_), channel_id=1, source_target_pairs={{0,8},{1,9},{2,10},{3,11},{4,12},{5,13},{6,14},{7,15},{8,0},{9,1},... | collective-permute-start | bytes 786440 | tf_op jit(solution)/shard_map/ppermute | solution.py:346
  34.5 7.9 %collective-permute-start.10 = (bf16[512,256]{1,0:T(8,128)(2,1)S(1)}, bf16[512,256]{1,0:T(8,128)(2,1)S(1)}, u32[]{:S(2)}, u32[]{:S(2)}) collective-permute-start(bf16[512,256]{1,0:T(8,128)(2,1)S(1)} %collective-permute-done.2.refs_5_), channel_id=1, source_target_pairs={{0,1},{1,0},{2,3},{3,2},{4,5},{5,4},{6,7},{7,6},{8,9},{9,8},{10,11... | collective-permute-start | bytes 786440 | tf_op jit(solution)/shard_map/ppermute | solution.py:349
  34.5 9.1 %collective-permute-start.16 = (bf16[512,256]{1,0:T(8,128)(2,1)S(1)}, bf16[512,256]{1,0:T(8,128)(2,1)}, u32[]{:S(2)}, u32[]{:S(2)}) collective-permute-start(bf16[512,256]{1,0:T(8,128)(2,1)S(1)} %collective-permute-done.8.refs_11_), channel_id=1, source_target_pairs={{0,1},{1,0},{2,3},{3,2},{4,5},{5,4},{6,7},{7,6},{8,9},{9,8},{10,11... | collective-permute-start | bytes 786440 | tf_op jit(solution)/shard_map/ppermute | solution.py:349
  42.3 1.7 %collective-permute-start.14 = (bf16[512,256]{1,0:T(8,128)(2,1)S(1)}, bf16[512,256]{1,0:T(8,128)(2,1)}, u32[]{:S(2)}, u32[]{:S(2)}) collective-permute-start(bf16[512,256]{1,0:T(8,128)(2,1)S(1)} %collective-permute-done.6.refs_9_), channel_id=1, source_target_pairs={{0,1},{1,0},{2,3},{3,2},{4,5},{5,4},{6,7},{7,6},{8,9},{9,8},{10,11... | collective-permute-start | bytes 786440 | tf_op jit(solution)/shard_map/ppermute | solution.py:349
  42.3 2.0 %collective-permute-start.15 = (bf16[512,256]{1,0:T(8,128)(2,1)S(1)}, bf16[512,256]{1,0:T(8,128)(2,1)}, u32[]{:S(2)}, u32[]{:S(2)}) collective-permute-start(bf16[512,256]{1,0:T(8,128)(2,1)S(1)} %collective-permute-done.7.refs_10_), channel_id=1, source_target_pairs={{0,1},{1,0},{2,3},{3,2},{4,5},{5,4},{6,7},{7,6},{8,9},{9,8},{10,11... | collective-permute-start | bytes 786440 | tf_op jit(solution)/shard_map/ppermute | solution.py:349
  87.3 3.6 %collective-permute-start.19 = (bf16[4,512,256]{2,1,0:T(8,128)(2,1)}, bf16[4,512,256]{2,1,0:T(8,128)(2,1)S(1)}, u32[]{:S(2)}, u32[]{:S(2)}) collective-permute-start(bf16[4,512,256]{2,1,0:T(8,128)(2,1)} %get-tuple-element.26), channel_id=1, source_target_pairs={{0,1},{1,0},{2,3},{3,2},{4,5},{5,4},{6,7},{7,6},{8,9},{9,8},{10,11... | collective-permute-start | bytes 3145736 | tf_op jit(solution)/shard_map/ppermute | solution.py:349
  87.5 8.7 %collective-permute-start.23 = (bf16[4,512,256]{2,1,0:T(8,128)(2,1)}, bf16[4,512,256]{2,1,0:T(8,128)(2,1)S(1)}, u32[]{:S(2)}, u32[]{:S(2)}) collective-permute-start(bf16[4,512,256]{2,1,0:T(8,128)(2,1)} %get-tuple-element.34), channel_id=1, source_target_pairs={{0,1},{1,0},{2,3},{3,2},{4,5},{5,4},{6,7},{7,6},{8,9},{9,8},{10,11... | collective-permute-start | bytes 3145736 | tf_op jit(solution)/shard_map/ppermute | solution.py:349
  87.9 56.6 %collective-permute-start.17 = (bf16[512,512]{1,0:T(8,128)(2,1)}, bf16[512,512]{1,0:T(8,128)(2,1)S(1)}, u32[]{:S(2)}, u32[]{:S(2)}) collective-permute-start(bf16[512,512]{1,0:T(8,128)(2,1)} %get-tuple-element.23), channel_id=1, source_target_pairs={{0,112},{1,113},{2,114},{3,115},{4,116},{5,117},{6,118},{7,119},{8... | collective-permute-start | bytes 1572872 | tf_op jit(solution)/shard_map/ppermute | solution.py:384
  90.9 53.6 %collective-permute-start.18 = (bf16[512,512]{1,0:T(8,128)(2,1)}, bf16[512,512]{1,0:T(8,128)(2,1)S(1)}, u32[]{:S(2)}, u32[]{:S(2)}) collective-permute-start(bf16[512,512]{1,0:T(8,128)(2,1)} %get-tuple-element.24), channel_id=1, source_target_pairs={{0,113},{1,112},{2,115},{3,114},{4,117},{5,116},{6,119},{7,118},{8... | collective-permute-start | bytes 1572872 | tf_op jit(solution)/shard_map/ppermute | solution.py:385
  91.2 38.7 %collective-permute-start.20 = (bf16[512,256]{1,0:T(8,128)(2,1)S(1)}, bf16[512,256]{1,0:T(8,128)(2,1)S(1)}, u32[]{:S(2)}, u32[]{:S(2)}) collective-permute-start(bf16[512,256]{1,0:T(8,128)(2,1)S(1)} %get-tuple-element.31), channel_id=1, source_target_pairs={{0,2},{1,3},{2,4},{3,5},{4,6},{5,7},{6,0},{7,1},{8,10},{9,11},{10,... | collective-permute-start | bytes 786440 | tf_op jit(solution)/shard_map/ppermute | solution.py:346
  96.2 36.9 %collective-permute-start.21 = (bf16[512,256]{1,0:T(8,128)(2,1)S(1)}, bf16[512,256]{1,0:T(8,128)(2,1)S(1)}, u32[]{:S(2)}, u32[]{:S(2)}) collective-permute-start(bf16[512,256]{1,0:T(8,128)(2,1)S(1)} %get-tuple-element.32), channel_id=1, source_target_pairs={{0,6},{1,7},{2,0},{3,1},{4,2},{5,3},{6,4},{7,5},{8,14},{9,15},{10,... | collective-permute-start | bytes 786440 | tf_op jit(solution)/shard_map/ppermute | solution.py:346
  96.3 32.9 %collective-permute-start.25 = (bf16[512,256]{1,0:T(8,128)(2,1)S(1)}, bf16[512,256]{1,0:T(8,128)(2,1)S(1)}, u32[]{:S(2)}, u32[]{:S(2)}) collective-permute-start(bf16[512,256]{1,0:T(8,128)(2,1)S(1)} %get-tuple-element.41), channel_id=1, source_target_pairs={{0,8},{1,9},{2,10},{3,11},{4,12},{5,13},{6,14},{7,15},{8,0},{9,1},... | collective-permute-start | bytes 786440 | tf_op jit(solution)/shard_map/ppermute | solution.py:346
  129.1 15.1 %collective-permute-start.24 = (bf16[512,256]{1,0:T(8,128)(2,1)S(1)}, bf16[512,256]{1,0:T(8,128)(2,1)S(1)}, u32[]{:S(2)}, u32[]{:S(2)}) collective-permute-start(bf16[512,256]{1,0:T(8,128)(2,1)S(1)} %get-tuple-element.38), channel_id=1, source_target_pairs={{0,2},{1,3},{2,4},{3,5},{4,6},{5,7},{6,0},{7,1},{8,10},{9,11},{10,... | collective-permute-start | bytes 786440 | tf_op jit(solution)/shard_map/ppermute | solution.py:346
  129.9 14.3 %collective-permute-start.27 = (bf16[512,256]{1,0:T(8,128)(2,1)S(1)}, bf16[512,256]{1,0:T(8,128)(2,1)S(1)}, u32[]{:S(2)}, u32[]{:S(2)}) collective-permute-start(bf16[512,256]{1,0:T(8,128)(2,1)S(1)} %get-tuple-element.42), channel_id=1, source_target_pairs={{0,6},{1,7},{2,0},{3,1},{4,2},{5,3},{6,4},{7,5},{8,14},{9,15},{10,... | collective-permute-start | bytes 786440 | tf_op jit(solution)/shard_map/ppermute | solution.py:346
  133.2 11.1 %collective-permute-start.26 = (bf16[512,256]{1,0:T(8,128)(2,1)}, bf16[512,256]{1,0:T(8,128)(2,1)S(1)}, u32[]{:S(2)}, u32[]{:S(2)}) collective-permute-start(bf16[512,256]{1,0:T(8,128)(2,1)} %fusion.1), channel_id=1, source_target_pairs={{0,4},{1,5},{2,6},{3,7},{4,0},{5,1},{6,2},{7,3},{8,12},{9,13},{10,... | collective-permute-start | bytes 786440 | tf_op jit(solution)/shard_map/ppermute | solution.py:346
  144.2 11.3 %collective-permute-start.22 = (bf16[512,256]{1,0:T(8,128)(2,1)S(1)}, bf16[512,256]{1,0:T(8,128)(2,1)S(1)}, u32[]{:S(2)}, u32[]{:S(2)}) collective-permute-start(bf16[512,256]{1,0:T(8,128)(2,1)S(1)} %add_convert_fusion.2), channel_id=1, source_target_pairs={{0,120},{1,121},{2,122},{3,123},{4,124},{5,125},{6,126},{7,127},{8... | collective-permute-start | bytes 786440 | tf_op jit(solution)/shard_map/ppermute | solution.py:402
  144.4 16.7 %collective-permute-start.28 = (bf16[512,256]{1,0:T(8,128)(2,1)S(1)}, bf16[512,256]{1,0:T(8,128)(2,1)S(1)}, u32[]{:S(2)}, u32[]{:S(2)}) collective-permute-start(bf16[512,256]{1,0:T(8,128)(2,1)S(1)} %add_convert_fusion.1), channel_id=1, source_target_pairs={{0,112},{1,113},{2,114},{3,115},{4,116},{5,117},{6,118},{7,119},{8... | collective-permute-start | bytes 786440 | tf_op jit(solution)/shard_map/ppermute | solution.py:402

commit v2 on v1

--- a/solution.py
+++ b/solution.py
@@ -326,7 +326,8 @@
             pltpu.SemaphoreType.DMA((1,)),
             pltpu.SemaphoreType.DMA((1,)),
         ],
-        compiler_params=pltpu.CompilerParams(vmem_limit_bytes=46 * 1024 * 1024),
+        compiler_params=pltpu.CompilerParams(vmem_limit_bytes=46 * 1024 * 1024,
+       ),
         name="attention",
     )(table, q_own, q_par, g_own, g_par, *pieces)
 
@@ -385,13 +386,9 @@
     dq_flip = lax.ppermute(dq_par, ("pipe", "ctx"), route(True))
     far = [total([own_parts[N_Z + i], far_swap[i]]).astype(jnp.bfloat16) for i in range(N_Z)]
     far = lax.optimization_barrier(far)
-    far2 = hop(far[2], 1, 0)
-    far1, far3 = hop(far[1], 0, 1), hop(far[3], 0, 3)
-    near = [total([own_parts[i], near_swap[i]]).astype(jnp.bfloat16) for i in (0, 1, 3)]
-    near0, near1, near3, near_swap = lax.optimization_barrier((*near, near_swap))
-    near1, near3 = hop(near1, 0, 1), hop(near3, 0, 3)
-    middle = total([own_parts[2], near_swap[2], far2]).astype(jnp.bfloat16)
-    near2 = hop(middle, 0, 2)
+    far_in = [hop(far[dz], 0, dz) for dz in (1, 2, 3)]
+    near = [total([own_parts[i], near_swap[i]]).astype(jnp.bfloat16) for i in range(N_Z)]
+    near_in = [hop(near[dz], 0, dz) for dz in (1, 2, 3)]
 
     def across(x, dy):
         pairs = []
@@ -401,8 +398,8 @@
                 pairs.append((s * n_ctx + i, to))
         return lax.ppermute(x, ("pipe", "ctx"), pairs)
 
-    crossed = across(total([far[0], far1, far3]).astype(jnp.bfloat16), 1)
-    straight = across(total([near0, near1, near2, near3]).astype(jnp.bfloat16), 0)
+    crossed = across(total([far[0]] + far_in).astype(jnp.bfloat16), 1)
+    straight = across(total([near[0]] + near_in).astype(jnp.bfloat16), 0)
     kv_out = total([crossed, straight]).astype(jnp.bfloat16)
     left = jnp.where(core == 0, dq_same, dq_flip)
     right = jnp.where(core == 0, dq_flip, dq_same)

time: 162 us -> 154 us (0.951)
  the two profiles are of different devices: /device:TPU:14 before, /device:TPU:6 now
where the time goes in v2:
time: 154 us; the launch traced here: 153 us
  waiting for transfers between devices  69.7 us (45%)
  Pallas kernels  50.8 us (33%)
  starting transfers between devices  24.2 us (16%)
  other arithmetic  6.57 us (4%)
    pallas_call x1, Pallas kernels, run_attention(): pl.pallas_call(functools.partial(attention_kernel, blocks=blocks, heads=h...  50.8 us
    ppermute x13, waiting for transfers between devices, hop(): return lax.ppermute(x, 'ctx', [(i, to(i)) for i in range(n_ctx)])  43.9 us
    ppermute x13, starting transfers between devices, hop(): return lax.ppermute(x, 'ctx', [(i, to(i)) for i in range(n_ctx)])  19.3 us
    ppermute x2, waiting for transfers between devices, across(): return lax.ppermute(x, ('pipe', 'ctx'), pairs)  11 us
    ppermute x1, waiting for transfers between devices, local(): dq_flip = lax.ppermute(dq_par, ('pipe', 'ctx'), route(True))  7.76 us
    ppermute x1, waiting for transfers between devices, local(): dq_same = lax.ppermute(dq_own, ('pipe', 'ctx'), route(False))  3.88 us
    ppermute x12, waiting for transfers between devices, swap(): return lax.ppermute(x, 'ctx', [(i, i ^ 1) for i in range(n_ctx)])  3.16 us
  transfers between devices with their start and end apart: 29, of which 14 were waited for; matrix products, arithmetic and copies ran while one was open for 4% of the time, Pallas kernels for 0%

profile of v2, /device:TPU:6, one launch (start us, length us, event | category | flops | bytes accessed | tf_op | source)
XLA Modules:
  0.0 153.5 jit_solution(14715699389619221752)
XLA Ops:
  0.6 1.0 pad_maximum_fusion.refs_4_
  1.6 3.3 %collective-permute-start.5 = (bf16[512,256]{1,0:T(8,128)(2,1)S(1)}, bf16[512,256]{1,0:T(8,128)(2,1)S(1)}, u32[]{:S(2)}, u32[]{:S(2)}) collective-permute-start(bf16[512,256]{1,0:T(8,128)(2,1)S(1)} %pad_maximum_fusion.refs_4_), channel_id=1, source_target_pairs={{0,8},{1,9},{2,10},{3,11},{4,12},{5,13},{6,14},{7,15},{8,0},{9,1},... | collective-permute-start | bytes 786440 | tf_op jit(solution)/shard_map/ppermute | solution.py:347
  4.9 4.0 %collective-permute-start.4 = (bf16[512,256]{1,0:T(8,128)(2,1)S(1)}, bf16[512,256]{1,0:T(8,128)(2,1)S(1)}, u32[]{:S(2)}, u32[]{:S(2)}) collective-permute-start(bf16[512,256]{1,0:T(8,128)(2,1)S(1)} %pad_maximum_fusion.refs_4_), channel_id=1, source_target_pairs={{0,6},{1,7},{2,0},{3,1},{4,2},{5,3},{6,4},{7,5},{8,14},{9,15},{10,... | collective-permute-start | bytes 786440 | tf_op jit(solution)/shard_map/ppermute | solution.py:347
  8.9 1.3 collective-permute-start.2
  10.2 1.1 collective-permute-done.5.refs_8_
  11.3 0.5 collective-permute-start
  11.8 9.0 %collective-permute-done.4.refs_7_ = bf16[512,256]{1,0:T(8,128)(2,1)S(1)} collective-permute-done((bf16[512,256]{1,0:T(8,128)(2,1)S(1)}, bf16[512,256]{1,0:T(8,128)(2,1)S(1)}, u32[]{:S(2)}, u32[]{:S(2)}) %collective-permute-start.4) | collective-permute-done | bytes 262176 | tf_op jit(solution)/shard_map/ppermute | solution.py:347
  20.8 3.7 %collective-permute-start.8 = (bf16[512,256]{1,0:T(8,128)(2,1)S(1)}, bf16[512,256]{1,0:T(8,128)(2,1)S(1)}, u32[]{:S(2)}, u32[]{:S(2)}) collective-permute-start(bf16[512,256]{1,0:T(8,128)(2,1)S(1)} %collective-permute-done.5.refs_8_), channel_id=1, source_target_pairs={{0,6},{1,7},{2,0},{3,1},{4,2},{5,3},{6,4},{7,5},{8,14},{9,15},{10,... | collective-permute-start | bytes 786440 | tf_op jit(solution)/shard_map/ppermute | solution.py:347
  24.8 5.9 %collective-permute-done.8.refs_11_ = bf16[512,256]{1,0:T(8,128)(2,1)S(1)} collective-permute-done((bf16[512,256]{1,0:T(8,128)(2,1)S(1)}, bf16[512,256]{1,0:T(8,128)(2,1)S(1)}, u32[]{:S(2)}, u32[]{:S(2)}) %collective-permute-start.8) | collective-permute-done | bytes 262176 | tf_op jit(solution)/shard_map/ppermute | solution.py:347
  30.7 3.4 %collective-permute-done.6.refs_9_ = bf16[512,256]{1,0:T(8,128)(2,1)S(1)} collective-permute-done((bf16[512,256]{1,0:T(8,128)(2,1)S(1)}, bf16[512,256]{1,0:T(8,128)(2,1)S(1)}, u32[]{:S(2)}, u32[]{:S(2)}) %collective-permute-start.6) | collective-permute-done | bytes 262176 | tf_op jit(solution)/shard_map/ppermute | solution.py:347
  35.0 8.2 %collective-permute-done.7.refs_10_ = bf16[512,256]{1,0:T(8,128)(2,1)S(1)} collective-permute-done((bf16[512,256]{1,0:T(8,128)(2,1)S(1)}, bf16[512,256]{1,0:T(8,128)(2,1)S(1)}, u32[]{:S(2)}, u32[]{:S(2)}) %collective-permute-start.7) | collective-permute-done | bytes 262176 | tf_op jit(solution)/shard_map/ppermute | solution.py:347
  43.2 0.5 collective-permute-start.15
  43.8 0.7 pad_add_fusion.table
  45.3 50.8 %attention.1 = (bf16[512,256]{1,0:T(8,128)(2,1)S(1)}, bf16[512,256]{1,0:T(8,128)(2,1)S(1)}, bf16[512,256]{1,0:T(8,128)(2,1)S(1)}, bf16[512,256]{1,0:T(8,128)(2,1...) custom-call(s32[25]{0:T(128)S(1)} %pad_add_fusion.table, ...), custom_call_target="tpu_custom_call" | custom-call | tf_op jit(solution)/shard_map/attention/pallas_call | solution.py:308
  96.7 2.4 %collective-permute-done.19 = bf16[4,512,256]{2,1,0:T(8,128)(2,1)S(1)} collective-permute-done((bf16[4,512,256]{2,1,0:T(8,128)(2,1)}, bf16[4,512,256]{2,1,0:T(8,128)(2,1)S(1)}, u32[]{:S(2)}, u32[]{:S(2)}) %collective-permute-start.19) | collective-permute-done | bytes 1048608 | tf_op jit(solution)/shard_map/ppermute | solution.py:350
  99.7 3.1 %collective-permute-start.22 = (bf16[512,256]{1,0:T(8,128)(2,1)S(1)}, bf16[512,256]{1,0:T(8,128)(2,1)S(1)}, u32[]{:S(2)}, u32[]{:S(2)}) collective-permute-start(bf16[512,256]{1,0:T(8,128)(2,1)S(1)} %get-tuple-element.29), channel_id=1, source_target_pairs={{0,6},{1,7},{2,0},{3,1},{4,2},{5,3},{6,4},{7,5},{8,14},{9,15},{10,... | collective-permute-start | bytes 786440 | tf_op jit(solution)/shard_map/ppermute | solution.py:347
  102.8 1.0 fusion.2
  103.8 0.9 collective-permute-start.25
  104.7 2.4 %collective-permute-start.27 = (bf16[512,256]{1,0:T(8,128)(2,1)}, bf16[512,256]{1,0:T(8,128)(2,1)}, u32[]{:S(2)}, u32[]{:S(2)}) collective-permute-start(bf16[512,256]{1,0:T(8,128)(2,1)} %get-tuple-element.40), channel_id=1, source_target_pairs={{0,6},{1,7},{2,0},{3,1},{4,2},{5,3},{6,4},{7,5},{8,14},{9,15},{10,... | collective-permute-start | bytes 786440 | tf_op jit(solution)/shard_map/ppermute | solution.py:347
  107.1 8.5 %collective-permute-done.20 = bf16[512,256]{1,0:T(8,128)(2,1)S(1)} collective-permute-done((bf16[512,256]{1,0:T(8,128)(2,1)S(1)}, bf16[512,256]{1,0:T(8,128)(2,1)S(1)}, u32[]{:S(2)}, u32[]{:S(2)}) %collective-permute-start.20) | collective-permute-done | bytes 262176 | tf_op jit(solution)/shard_map/ppermute | solution.py:347
  115.6 1.0 collective-permute-start.17
  116.6 0.7 copy-done.2
  117.3 1.1 add_convert_fusion.2
  118.4 7.7 %collective-permute-done.25 = bf16[512,256]{1,0:T(8,128)(2,1)} collective-permute-done((bf16[512,256]{1,0:T(8,128)(2,1)}, bf16[512,256]{1,0:T(8,128)(2,1)}, u32[]{:S(2)}, u32[]{:S(2)}) %collective-permute-start.25) | collective-permute-done | bytes 262176 | tf_op jit(solution)/shard_map/ppermute | solution.py:347
  126.1 1.3 add_convert_fusion.1
  127.4 1.4 collective-permute-start.28
  128.8 3.9 %collective-permute-done.17 = bf16[512,512]{1,0:T(8,128)(2,1)S(1)} collective-permute-done((bf16[512,512]{1,0:T(8,128)(2,1)}, bf16[512,512]{1,0:T(8,128)(2,1)S(1)}, u32[]{:S(2)}, u32[]{:S(2)}) %collective-permute-start.17) | collective-permute-done | bytes 524320 | tf_op jit(solution)/shard_map/ppermute | solution.py:385
  132.7 7.8 %collective-permute-done.18 = bf16[512,512]{1,0:T(8,128)(2,1)S(1)} collective-permute-done((bf16[512,512]{1,0:T(8,128)(2,1)}, bf16[512,512]{1,0:T(8,128)(2,1)S(1)}, u32[]{:S(2)}, u32[]{:S(2)}) %collective-permute-start.18) | collective-permute-done | bytes 524320 | tf_op jit(solution)/shard_map/ppermute | solution.py:386
  140.6 1.1 maximum_bitcast_fusion
  141.7 7.3 %collective-permute-done.23 = bf16[512,256]{1,0:T(8,128)(2,1)S(1)} collective-permute-done((bf16[512,256]{1,0:T(8,128)(2,1)S(1)}, bf16[512,256]{1,0:T(8,128)(2,1)S(1)}, u32[]{:S(2)}, u32[]{:S(2)}) %collective-permute-start.23) | collective-permute-done | bytes 262176 | tf_op jit(solution)/shard_map/ppermute | solution.py:399
  149.0 3.7 %collective-permute-done.28 = bf16[512,256]{1,0:T(8,128)(2,1)S(1)} collective-permute-done((bf16[512,256]{1,0:T(8,128)(2,1)S(1)}, bf16[512,256]{1,0:T(8,128)(2,1)S(1)}, u32[]{:S(2)}, u32[]{:S(2)}) %collective-permute-start.28) | collective-permute-done | bytes 262176 | tf_op jit(solution)/shard_map/ppermute | solution.py:399
  152.7 0.7 slice_bitcast_fusion.8
  (43 shorter events, 3.3 us)
Async XLA Ops:
  1.6 9.6 %collective-permute-start.5 = (bf16[512,256]{1,0:T(8,128)(2,1)S(1)}, bf16[512,256]{1,0:T(8,128)(2,1)S(1)}, u32[]{:S(2)}, u32[]{:S(2)}) collective-permute-start(bf16[512,256]{1,0:T(8,128)(2,1)S(1)} %pad_maximum_fusion.refs_4_), channel_id=1, source_target_pairs={{0,8},{1,9},{2,10},{3,11},{4,12},{5,13},{6,14},{7,15},{8,0},{9,1},... | collective-permute-start | bytes 786440 | tf_op jit(solution)/shard_map/ppermute | solution.py:347
  4.9 6.4 %collective-permute-start.9 = (bf16[512,256]{1,0:T(8,128)(2,1)S(1)}, bf16[512,256]{1,0:T(8,128)(2,1)S(1)}, u32[]{:S(2)}, u32[]{:S(2)}) collective-permute-start(bf16[512,256]{1,0:T(8,128)(2,1)S(1)} %pad_maximum_fusion.refs_4_), channel_id=1, source_target_pairs={{0,1},{1,0},{2,3},{3,2},{4,5},{5,4},{6,7},{7,6},{8,9},{9,8},{10,11... | collective-permute-start | bytes 786440 | tf_op jit(solution)/shard_map/ppermute | solution.py:350
  4.9 15.9 %collective-permute-start.4 = (bf16[512,256]{1,0:T(8,128)(2,1)S(1)}, bf16[512,256]{1,0:T(8,128)(2,1)S(1)}, u32[]{:S(2)}, u32[]{:S(2)}) collective-permute-start(bf16[512,256]{1,0:T(8,128)(2,1)S(1)} %pad_maximum_fusion.refs_4_), channel_id=1, source_target_pairs={{0,6},{1,7},{2,0},{3,1},{4,2},{5,3},{6,4},{7,5},{8,14},{9,15},{10,... | collective-permute-start | bytes 786440 | tf_op jit(solution)/shard_map/ppermute | solution.py:347
  8.9 11.9 %collective-permute-start.3 = (bf16[512,256]{1,0:T(8,128)(2,1)S(1)}, bf16[512,256]{1,0:T(8,128)(2,1)S(1)}, u32[]{:S(2)}, u32[]{:S(2)}) collective-permute-start(bf16[512,256]{1,0:T(8,128)(2,1)S(1)} %pad_maximum_fusion.refs_4_), channel_id=1, source_target_pairs={{0,4},{1,5},{2,6},{3,7},{4,0},{5,1},{6,2},{7,3},{8,12},{9,13},{10,... | collective-permute-start | bytes 786440 | tf_op jit(solution)/shard_map/ppermute | solution.py:347
  8.9 15.6 %collective-permute-start.2 = (bf16[512,256]{1,0:T(8,128)(2,1)S(1)}, bf16[512,256]{1,0:T(8,128)(2,1)S(1)}, u32[]{:S(2)}, u32[]{:S(2)}) collective-permute-start(bf16[512,256]{1,0:T(8,128)(2,1)S(1)} %pad_maximum_fusion.refs_4_), channel_id=1, source_target_pairs={{0,2},{1,3},{2,4},{3,5},{4,6},{5,7},{6,0},{7,1},{8,10},{9,11},{10,... | collective-permute-start | bytes 786440 | tf_op jit(solution)/shard_map/ppermute | solution.py:347
  11.3 13.2 %collective-permute-start.13 = (bf16[512,256]{1,0:T(8,128)(2,1)S(1)}, bf16[512,256]{1,0:T(8,128)(2,1)S(1)}, u32[]{:S(2)}, u32[]{:S(2)}) collective-permute-start(bf16[512,256]{1,0:T(8,128)(2,1)S(1)} %collective-permute-done.5.refs_8_), channel_id=1, source_target_pairs={{0,1},{1,0},{2,3},{3,2},{4,5},{5,4},{6,7},{7,6},{8,9},{9,8},{10,11... | collective-permute-start | bytes 786440 | tf_op jit(solution)/shard_map/ppermute | solution.py:350
  11.3 34.0 %collective-permute-start = (bf16[512,1024]{1,0:T(8,128)(2,1)}, bf16[512,1024]{1,0:T(8,128)(2,1)}, u32[]{:S(2)}, u32[]{:S(2)}) collective-permute-start(bf16[512,1024]{1,0:T(8,128)(2,1)} %bitcast.53), channel_id=1, source_target_pairs={{0,1},{1,0},{2,3},{3,2},{4,5},{5,4},{6,7},{7,6},{8,9},{9,8},{10,11... | collective-permute-start | bytes 3145736 | tf_op jit(solution)/shard_map/ppermute | solution.py:350
  20.8 24.5 %collective-permute-start.1 = (bf16[512,1024]{1,0:T(8,128)(2,1)}, bf16[512,1024]{1,0:T(8,128)(2,1)}, u32[]{:S(2)}, u32[]{:S(2)}) collective-permute-start(bf16[512,1024]{1,0:T(8,128)(2,1)} %bitcast.55), channel_id=1, source_target_pairs={{0,1},{1,0},{2,3},{3,2},{4,5},{5,4},{6,7},{7,6},{8,9},{9,8},{10,11... | collective-permute-start | bytes 3145736 | tf_op jit(solution)/shard_map/ppermute | solution.py:350
  20.8 9.9 %collective-permute-start.8 = (bf16[512,256]{1,0:T(8,128)(2,1)S(1)}, bf16[512,256]{1,0:T(8,128)(2,1)S(1)}, u32[]{:S(2)}, u32[]{:S(2)}) collective-permute-start(bf16[512,256]{1,0:T(8,128)(2,1)S(1)} %collective-permute-done.5.refs_8_), channel_id=1, source_target_pairs={{0,6},{1,7},{2,0},{3,1},{4,2},{5,3},{6,4},{7,5},{8,14},{9,15},{10,... | collective-permute-start | bytes 786440 | tf_op jit(solution)/shard_map/ppermute | solution.py:347
  24.5 9.6 %collective-permute-start.6 = (bf16[512,256]{1,0:T(8,128)(2,1)S(1)}, bf16[512,256]{1,0:T(8,128)(2,1)S(1)}, u32[]{:S(2)}, u32[]{:S(2)}) collective-permute-start(bf16[512,256]{1,0:T(8,128)(2,1)S(1)} %collective-permute-done.5.refs_8_), channel_id=1, source_target_pairs={{0,2},{1,3},{2,4},{3,5},{4,6},{5,7},{6,0},{7,1},{8,10},{9,11},{10,... | collective-permute-start | bytes 786440 | tf_op jit(solution)/shard_map/ppermute | solution.py:347
  24.5 10.0 %collective-permute-start.12 = (bf16[512,256]{1,0:T(8,128)(2,1)S(1)}, bf16[512,256]{1,0:T(8,128)(2,1)S(1)}, u32[]{:S(2)}, u32[]{:S(2)}) collective-permute-start(bf16[512,256]{1,0:T(8,128)(2,1)S(1)} %collective-permute-done.4.refs_7_), channel_id=1, source_target_pairs={{0,1},{1,0},{2,3},{3,2},{4,5},{5,4},{6,7},{7,6},{8,9},{9,8},{10,11... | collective-permute-start | bytes 786440 | tf_op jit(solution)/shard_map/ppermute | solution.py:350
  30.7 3.8 %collective-permute-start.11 = (bf16[512,256]{1,0:T(8,128)(2,1)S(1)}, bf16[512,256]{1,0:T(8,128)(2,1)S(1)}, u32[]{:S(2)}, u32[]{:S(2)}) collective-permute-start(bf16[512,256]{1,0:T(8,128)(2,1)S(1)} %collective-permute-done.3.refs_6_), channel_id=1, source_target_pairs={{0,1},{1,0},{2,3},{3,2},{4,5},{5,4},{6,7},{7,6},{8,9},{9,8},{10,11... | collective-permute-start | bytes 786440 | tf_op jit(solution)/shard_map/ppermute | solution.py:350
  34.2 9.1 %collective-permute-start.7 = (bf16[512,256]{1,0:T(8,128)(2,1)S(1)}, bf16[512,256]{1,0:T(8,128)(2,1)S(1)}, u32[]{:S(2)}, u32[]{:S(2)}) collective-permute-start(bf16[512,256]{1,0:T(8,128)(2,1)S(1)} %collective-permute-done.3.refs_6_), channel_id=1, source_target_pairs={{0,8},{1,9},{2,10},{3,11},{4,12},{5,13},{6,14},{7,15},{8,0},{9,1},... | collective-permute-start | bytes 786440 | tf_op jit(solution)/shard_map/ppermute | solution.py:347
  34.5 8.8 %collective-permute-start.10 = (bf16[512,256]{1,0:T(8,128)(2,1)S(1)}, bf16[512,256]{1,0:T(8,128)(2,1)S(1)}, u32[]{:S(2)}, u32[]{:S(2)}) collective-permute-start(bf16[512,256]{1,0:T(8,128)(2,1)S(1)} %collective-permute-done.2.refs_5_), channel_id=1, source_target_pairs={{0,1},{1,0},{2,3},{3,2},{4,5},{5,4},{6,7},{7,6},{8,9},{9,8},{10,11... | collective-permute-start | bytes 786440 | tf_op jit(solution)/shard_map/ppermute | solution.py:350
  34.5 10.0 %collective-permute-start.16 = (bf16[512,256]{1,0:T(8,128)(2,1)S(1)}, bf16[512,256]{1,0:T(8,128)(2,1)}, u32[]{:S(2)}, u32[]{:S(2)}) collective-permute-start(bf16[512,256]{1,0:T(8,128)(2,1)S(1)} %collective-permute-done.8.refs_11_), channel_id=1, source_target_pairs={{0,1},{1,0},{2,3},{3,2},{4,5},{5,4},{6,7},{7,6},{8,9},{9,8},{10,11... | collective-permute-start | bytes 786440 | tf_op jit(solution)/shard_map/ppermute | solution.py:350
  43.2 1.7 %collective-permute-start.14 = (bf16[512,256]{1,0:T(8,128)(2,1)S(1)}, bf16[512,256]{1,0:T(8,128)(2,1)}, u32[]{:S(2)}, u32[]{:S(2)}) collective-permute-start(bf16[512,256]{1,0:T(8,128)(2,1)S(1)} %collective-permute-done.6.refs_9_), channel_id=1, source_target_pairs={{0,1},{1,0},{2,3},{3,2},{4,5},{5,4},{6,7},{7,6},{8,9},{9,8},{10,11... | collective-permute-start | bytes 786440 | tf_op jit(solution)/shard_map/ppermute | solution.py:350
  43.2 2.0 %collective-permute-start.15 = (bf16[512,256]{1,0:T(8,128)(2,1)S(1)}, bf16[512,256]{1,0:T(8,128)(2,1)}, u32[]{:S(2)}, u32[]{:S(2)}) collective-permute-start(bf16[512,256]{1,0:T(8,128)(2,1)S(1)} %collective-permute-done.7.refs_10_), channel_id=1, source_target_pairs={{0,1},{1,0},{2,3},{3,2},{4,5},{5,4},{6,7},{7,6},{8,9},{9,8},{10,11... | collective-permute-start | bytes 786440 | tf_op jit(solution)/shard_map/ppermute | solution.py:350
  96.1 3.2 %copy-start = (bf16[512,256]{1,0:T(8,128)(2,1)}, bf16[512,256]{1,0:T(8,128)(2,1)S(1)}, u32[]{:S(2)}) copy-start(bf16[512,256]{1,0:T(8,128)(2,1)S(1)} %get-tuple-element.30) | copy-start | bytes 786436
  96.1 3.0 %collective-permute-start.19 = (bf16[4,512,256]{2,1,0:T(8,128)(2,1)}, bf16[4,512,256]{2,1,0:T(8,128)(2,1)S(1)}, u32[]{:S(2)}, u32[]{:S(2)}) collective-permute-start(bf16[4,512,256]{2,1,0:T(8,128)(2,1)} %get-tuple-element.22), channel_id=1, source_target_pairs={{0,1},{1,0},{2,3},{3,2},{4,5},{5,4},{6,7},{7,6},{8,9},{9,8},{10,11... | collective-permute-start | bytes 3145736 | tf_op jit(solution)/shard_map/ppermute | solution.py:350
  96.3 6.5 %collective-permute-start.24 = (bf16[4,512,256]{2,1,0:T(8,128)(2,1)}, bf16[4,512,256]{2,1,0:T(8,128)(2,1)S(1)}, u32[]{:S(2)}, u32[]{:S(2)}) collective-permute-start(bf16[4,512,256]{2,1,0:T(8,128)(2,1)} %get-tuple-element.31), channel_id=1, source_target_pairs={{0,1},{1,0},{2,3},{3,2},{4,5},{5,4},{6,7},{7,6},{8,9},{9,8},{10,11... | collective-permute-start | bytes 3145736 | tf_op jit(solution)/shard_map/ppermute | solution.py:350
  99.3 16.3 %collective-permute-start.20 = (bf16[512,256]{1,0:T(8,128)(2,1)S(1)}, bf16[512,256]{1,0:T(8,128)(2,1)S(1)}, u32[]{:S(2)}, u32[]{:S(2)}) collective-permute-start(bf16[512,256]{1,0:T(8,128)(2,1)S(1)} %get-tuple-element.27), channel_id=1, source_target_pairs={{0,2},{1,3},{2,4},{3,5},{4,6},{5,7},{6,0},{7,1},{8,10},{9,11},{10,... | collective-permute-start | bytes 786440 | tf_op jit(solution)/shard_map/ppermute | solution.py:347
  99.6 16.0 %collective-permute-start.21 = (bf16[512,256]{1,0:T(8,128)(2,1)S(1)}, bf16[512,256]{1,0:T(8,128)(2,1)S(1)}, u32[]{:S(2)}, u32[]{:S(2)}) collective-permute-start(bf16[512,256]{1,0:T(8,128)(2,1)S(1)} %get-tuple-element.28), channel_id=1, source_target_pairs={{0,4},{1,5},{2,6},{3,7},{4,0},{5,1},{6,2},{7,3},{8,12},{9,13},{10,... | collective-permute-start | bytes 786440 | tf_op jit(solution)/shard_map/ppermute | solution.py:347
  99.7 16.9 %collective-permute-start.22 = (bf16[512,256]{1,0:T(8,128)(2,1)S(1)}, bf16[512,256]{1,0:T(8,128)(2,1)S(1)}, u32[]{:S(2)}, u32[]{:S(2)}) collective-permute-start(bf16[512,256]{1,0:T(8,128)(2,1)S(1)} %get-tuple-element.29), channel_id=1, source_target_pairs={{0,6},{1,7},{2,0},{3,1},{4,2},{5,3},{6,4},{7,5},{8,14},{9,15},{10,... | collective-permute-start | bytes 786440 | tf_op jit(solution)/shard_map/ppermute | solution.py:347
  103.8 22.3 %copy-start.1 = (bf16[512,256]{1,0:T(8,128)(2,1)S(1)}, bf16[512,256]{1,0:T(8,128)(2,1)}, u32[]{:S(2)}) copy-start(bf16[512,256]{1,0:T(8,128)(2,1)} %copy-done) | copy-start | bytes 786436
  103.8 22.3 %collective-permute-start.25 = (bf16[512,256]{1,0:T(8,128)(2,1)}, bf16[512,256]{1,0:T(8,128)(2,1)}, u32[]{:S(2)}, u32[]{:S(2)}) collective-permute-start(bf16[512,256]{1,0:T(8,128)(2,1)} %get-tuple-element.39), channel_id=1, source_target_pairs={{0,2},{1,3},{2,4},{3,5},{4,6},{5,7},{6,0},{7,1},{8,10},{9,11},{10,... | collective-permute-start | bytes 786440 | tf_op jit(solution)/shard_map/ppermute | solution.py:347
  104.7 21.4 %collective-permute-start.27 = (bf16[512,256]{1,0:T(8,128)(2,1)}, bf16[512,256]{1,0:T(8,128)(2,1)}, u32[]{:S(2)}, u32[]{:S(2)}) collective-permute-start(bf16[512,256]{1,0:T(8,128)(2,1)} %get-tuple-element.40), channel_id=1, source_target_pairs={{0,6},{1,7},{2,0},{3,1},{4,2},{5,3},{6,4},{7,5},{8,14},{9,15},{10,... | collective-permute-start | bytes 786440 | tf_op jit(solution)/shard_map/ppermute | solution.py:347
  115.6 10.5 %collective-permute-start.26 = (bf16[512,256]{1,0:T(8,128)(2,1)S(1)}, bf16[512,256]{1,0:T(8,128)(2,1)}, u32[]{:S(2)}, u32[]{:S(2)}) collective-permute-start(bf16[512,256]{1,0:T(8,128)(2,1)S(1)} %get-tuple-element.41), channel_id=1, source_target_pairs={{0,4},{1,5},{2,6},{3,7},{4,0},{5,1},{6,2},{7,3},{8,12},{9,13},{10,... | collective-permute-start | bytes 786440 | tf_op jit(solution)/shard_map/ppermute | solution.py:347
  115.6 17.1 %collective-permute-start.17 = (bf16[512,512]{1,0:T(8,128)(2,1)}, bf16[512,512]{1,0:T(8,128)(2,1)S(1)}, u32[]{:S(2)}, u32[]{:S(2)}) collective-permute-start(bf16[512,512]{1,0:T(8,128)(2,1)} %get-tuple-element.19), channel_id=1, source_target_pairs={{0,112},{1,113},{2,114},{3,115},{4,116},{5,117},{6,118},{7,119},{8... | collective-permute-start | bytes 1572872 | tf_op jit(solution)/shard_map/ppermute | solution.py:385
  116.6 0.7 copy-start.2
  117.3 23.2 %collective-permute-start.18 = (bf16[512,512]{1,0:T(8,128)(2,1)}, bf16[512,512]{1,0:T(8,128)(2,1)S(1)}, u32[]{:S(2)}, u32[]{:S(2)}) collective-permute-start(bf16[512,512]{1,0:T(8,128)(2,1)} %get-tuple-element.20), channel_id=1, source_target_pairs={{0,113},{1,112},{2,115},{3,114},{4,117},{5,116},{6,119},{7,118},{8... | collective-permute-start | bytes 1572872 | tf_op jit(solution)/shard_map/ppermute | solution.py:386
  126.1 22.9 %collective-permute-start.23 = (bf16[512,256]{1,0:T(8,128)(2,1)S(1)}, bf16[512,256]{1,0:T(8,128)(2,1)S(1)}, u32[]{:S(2)}, u32[]{:S(2)}) collective-permute-start(bf16[512,256]{1,0:T(8,128)(2,1)S(1)} %add_convert_fusion.2), channel_id=1, source_target_pairs={{0,120},{1,121},{2,122},{3,123},{4,124},{5,125},{6,126},{7,127},{8... | collective-permute-start | bytes 786440 | tf_op jit(solution)/shard_map/ppermute | solution.py:399
  127.4 25.3 %collective-permute-start.28 = (bf16[512,256]{1,0:T(8,128)(2,1)S(1)}, bf16[512,256]{1,0:T(8,128)(2,1)S(1)}, u32[]{:S(2)}, u32[]{:S(2)}) collective-permute-start(bf16[512,256]{1,0:T(8,128)(2,1)S(1)} %add_convert_fusion.1), channel_id=1, source_target_pairs={{0,112},{1,113},{2,114},{3,115},{4,116},{5,117},{6,118},{7,119},{8... | collective-permute-start | bytes 786440 | tf_op jit(solution)/shard_map/ppermute | solution.py:399

commit v3 on v2

--- a/solution.py
+++ b/solution.py
@@ -210,10 +210,10 @@
     zero = jnp.zeros((8, BLK), jnp.float32)
     fresh = (none, zero, zero)
 
-    def sweep(low, high, body, state):
-        pairs = (high - low) // 2
-        state = lax.fori_loop(0, pairs, lambda t, st: body(low + 2 * t, 2, st), state)
-        return lax.fori_loop(low + 2 * pairs, high, lambda t, st: body(t, 1, st), state)
+    def sweep(low, high, body, state, size=2):
+        full = (high - low) // size
+        state = lax.fori_loop(0, full, lambda t, st: body(low + size * t, size, st), state)
+        return lax.fori_loop(low + size * full, high, lambda t, st: body(t, 1, st), state)
 
     def start():
         b, lo, count = span(0)
@@ -231,15 +231,15 @@
         b, lo, count = span(i)
         b_n, lo_n, count_n = span(nxt)
         todo = jnp.where(i + 1 < items, count_n, 0)
-        both = jnp.minimum(count, todo) // 2
+        both = jnp.minimum(count, todo)
         prepare(nxt, b_n, later)
         dqt[...] = jnp.zeros_like(dqt)
         state = stats(b_n, count_n, later, fresh, True, 1)
         grads(b, count, now, n, h, final, 1)
 
-        def joint(t, state):
-            state = stats(lo_n + 2 * t, 2 * t, later, state, False, 2)
-            grads(lo + 2 * t, 2 * t, now, n, h, final, 2)
+        def joint(t, size, state):
+            state = stats(lo_n + t, t, later, state, False, size)
+            grads(lo + t, t, now, n, h, final, size)
             return state
 
         def ahead(t, size, state):
@@ -249,9 +249,9 @@
             grads(lo + t, t, now, n, h, final, size)
             return carry
 
-        state = lax.fori_loop(0, both, joint, state)
-        state = sweep(2 * both, todo, ahead, state)
-        sweep(2 * both, count, behind, 0)
+        state = sweep(0, both, joint, state, 3)
+        state = sweep(both, todo, ahead, state)
+        sweep(both, count, behind, 0)
         dq[n, h] = (dqt[...] * SCALE).T.astype(jnp.bfloat16)
         return finish(state)
 

time: 154 us -> 151 us (0.981)
  Pallas kernels: 50.8 us -> 48.4 us
  waiting for transfers between devices: 69.7 us -> 71.7 us
  starting transfers between devices: 24.2 us -> 22.4 us
    pallas_call x1, Pallas kernels: 50.8 us -> 48.4 us  [run_attention(): pl.pallas_call(functools.partial(attention_kernel, blocks=blocks, heads=h...]
  transfers between devices with their start and end apart: 29 -> 29, of which waited for: 14 -> 15; matrix products, arithmetic and copies ran while one was open for 4% -> 4% of each run, Pallas kernels for 0% -> 0%
where the time goes in v3:
time: 151 us
  waiting for transfers between devices  71.7 us (47%)
  Pallas kernels  48.4 us (32%)
  starting transfers between devices  22.4 us (15%)
  other arithmetic  6.57 us (4%)
    pallas_call x1, Pallas kernels, run_attention(): pl.pallas_call(functools.partial(attention_kernel, blocks=blocks, heads=h...  48.4 us
    ppermute x13, waiting for transfers between devices, hop(): return lax.ppermute(x, 'ctx', [(i, to(i)) for i in range(n_ctx)])  44.7 us
    ppermute x13, starting transfers between devices, hop(): return lax.ppermute(x, 'ctx', [(i, to(i)) for i in range(n_ctx)])  19.1 us
    ppermute x2, waiting for transfers between devices, across(): return lax.ppermute(x, ('pipe', 'ctx'), pairs)  12.1 us
    ppermute x1, waiting for transfers between devices, local(): dq_flip = lax.ppermute(dq_par, ('pipe', 'ctx'), route(True))  7.1 us
    ppermute x1, waiting for transfers between devices, local(): dq_same = lax.ppermute(dq_own, ('pipe', 'ctx'), route(False))  4.67 us
    ppermute x12, waiting for transfers between devices, swap(): return lax.ppermute(x, 'ctx', [(i, i ^ 1) for i in range(n_ctx)])  3.16 us
  transfers between devices with their start and end apart: 29, of which 15 were waited for; matrix products, arithmetic and copies ran while one was open for 4% of the time, Pallas kernels for 0%

profile of v3, /device:TPU:6, one launch (start us, length us, event | category | flops | bytes accessed | tf_op | source)
XLA Modules:
  0.0 151.2 jit_solution(8545178286872650533)
XLA Ops:
  0.6 1.0 pad_maximum_fusion.refs_4_
  1.6 3.3 %collective-permute-start.5 = (bf16[512,256]{1,0:T(8,128)(2,1)S(1)}, bf16[512,256]{1,0:T(8,128)(2,1)S(1)}, u32[]{:S(2)}, u32[]{:S(2)}) collective-permute-start(bf16[512,256]{1,0:T(8,128)(2,1)S(1)} %pad_maximum_fusion.refs_4_), channel_id=1, source_target_pairs={{0,8},{1,9},{2,10},{3,11},{4,12},{5,13},{6,14},{7,15},{8,0},{9,1},... | collective-permute-start | bytes 786440 | tf_op jit(solution)/shard_map/ppermute | solution.py:347
  4.9 4.0 %collective-permute-start.4 = (bf16[512,256]{1,0:T(8,128)(2,1)S(1)}, bf16[512,256]{1,0:T(8,128)(2,1)S(1)}, u32[]{:S(2)}, u32[]{:S(2)}) collective-permute-start(bf16[512,256]{1,0:T(8,128)(2,1)S(1)} %pad_maximum_fusion.refs_4_), channel_id=1, source_target_pairs={{0,6},{1,7},{2,0},{3,1},{4,2},{5,3},{6,4},{7,5},{8,14},{9,15},{10,... | collective-permute-start | bytes 786440 | tf_op jit(solution)/shard_map/ppermute | solution.py:347
  8.9 1.3 collective-permute-start.2
  10.2 1.1 collective-permute-done.5.refs_8_
  11.3 0.5 collective-permute-start
  11.8 9.0 %collective-permute-done.4.refs_7_ = bf16[512,256]{1,0:T(8,128)(2,1)S(1)} collective-permute-done((bf16[512,256]{1,0:T(8,128)(2,1)S(1)}, bf16[512,256]{1,0:T(8,128)(2,1)S(1)}, u32[]{:S(2)}, u32[]{:S(2)}) %collective-permute-start.4) | collective-permute-done | bytes 262176 | tf_op jit(solution)/shard_map/ppermute | solution.py:347
  20.8 3.7 %collective-permute-start.8 = (bf16[512,256]{1,0:T(8,128)(2,1)S(1)}, bf16[512,256]{1,0:T(8,128)(2,1)S(1)}, u32[]{:S(2)}, u32[]{:S(2)}) collective-permute-start(bf16[512,256]{1,0:T(8,128)(2,1)S(1)} %collective-permute-done.5.refs_8_), channel_id=1, source_target_pairs={{0,6},{1,7},{2,0},{3,1},{4,2},{5,3},{6,4},{7,5},{8,14},{9,15},{10,... | collective-permute-start | bytes 786440 | tf_op jit(solution)/shard_map/ppermute | solution.py:347
  24.8 5.9 %collective-permute-done.8.refs_11_ = bf16[512,256]{1,0:T(8,128)(2,1)S(1)} collective-permute-done((bf16[512,256]{1,0:T(8,128)(2,1)S(1)}, bf16[512,256]{1,0:T(8,128)(2,1)S(1)}, u32[]{:S(2)}, u32[]{:S(2)}) %collective-permute-start.8) | collective-permute-done | bytes 262176 | tf_op jit(solution)/shard_map/ppermute | solution.py:347
  30.7 3.4 %collective-permute-done.6.refs_9_ = bf16[512,256]{1,0:T(8,128)(2,1)S(1)} collective-permute-done((bf16[512,256]{1,0:T(8,128)(2,1)S(1)}, bf16[512,256]{1,0:T(8,128)(2,1)S(1)}, u32[]{:S(2)}, u32[]{:S(2)}) %collective-permute-start.6) | collective-permute-done | bytes 262176 | tf_op jit(solution)/shard_map/ppermute | solution.py:347
  34.5 0.5 collective-permute-start.16
  35.0 8.2 %collective-permute-done.7.refs_10_ = bf16[512,256]{1,0:T(8,128)(2,1)S(1)} collective-permute-done((bf16[512,256]{1,0:T(8,128)(2,1)S(1)}, bf16[512,256]{1,0:T(8,128)(2,1)S(1)}, u32[]{:S(2)}, u32[]{:S(2)}) %collective-permute-start.7) | collective-permute-done | bytes 262176 | tf_op jit(solution)/shard_map/ppermute | solution.py:347
  43.2 0.5 collective-permute-start.15
  43.8 0.7 pad_add_fusion.table
  45.3 48.4 %attention.1 = (bf16[512,256]{1,0:T(8,128)(2,1)S(1)}, bf16[512,256]{1,0:T(8,128)(2,1)S(1)}, bf16[512,256]{1,0:T(8,128)(2,1)S(1)}, bf16[512,256]{1,0:T(8,128)(2,1...) custom-call(s32[25]{0:T(128)S(1)} %pad_add_fusion.table, ...), custom_call_target="tpu_custom_call" | custom-call | tf_op jit(solution)/shard_map/attention/pallas_call | solution.py:308
  94.4 2.4 %collective-permute-done.19 = bf16[4,512,256]{2,1,0:T(8,128)(2,1)S(1)} collective-permute-done((bf16[4,512,256]{2,1,0:T(8,128)(2,1)}, bf16[4,512,256]{2,1,0:T(8,128)(2,1)S(1)}, u32[]{:S(2)}, u32[]{:S(2)}) %collective-permute-start.19) | collective-permute-done | bytes 1048608 | tf_op jit(solution)/shard_map/ppermute | solution.py:350
  97.2 3.1 %collective-permute-start.22 = (bf16[512,256]{1,0:T(8,128)(2,1)S(1)}, bf16[512,256]{1,0:T(8,128)(2,1)S(1)}, u32[]{:S(2)}, u32[]{:S(2)}) collective-permute-start(bf16[512,256]{1,0:T(8,128)(2,1)S(1)} %get-tuple-element.29), channel_id=1, source_target_pairs={{0,6},{1,7},{2,0},{3,1},{4,2},{5,3},{6,4},{7,5},{8,14},{9,15},{10,... | collective-permute-start | bytes 786440 | tf_op jit(solution)/shard_map/ppermute | solution.py:347
  100.4 1.0 fusion.2
  101.4 0.9 collective-permute-start.25
  102.2 2.4 %collective-permute-start.27 = (bf16[512,256]{1,0:T(8,128)(2,1)}, bf16[512,256]{1,0:T(8,128)(2,1)}, u32[]{:S(2)}, u32[]{:S(2)}) collective-permute-start(bf16[512,256]{1,0:T(8,128)(2,1)} %get-tuple-element.40), channel_id=1, source_target_pairs={{0,6},{1,7},{2,0},{3,1},{4,2},{5,3},{6,4},{7,5},{8,14},{9,15},{10,... | collective-permute-start | bytes 786440 | tf_op jit(solution)/shard_map/ppermute | solution.py:347
  104.6 8.3 %collective-permute-done.20 = bf16[512,256]{1,0:T(8,128)(2,1)S(1)} collective-permute-done((bf16[512,256]{1,0:T(8,128)(2,1)S(1)}, bf16[512,256]{1,0:T(8,128)(2,1)S(1)}, u32[]{:S(2)}, u32[]{:S(2)}) %collective-permute-start.20) | collective-permute-done | bytes 262176 | tf_op jit(solution)/shard_map/ppermute | solution.py:347
  113.1 0.8 collective-permute-done.22
  114.0 0.7 copy-done.2
  114.7 1.1 add_convert_fusion.2
  115.8 7.9 %collective-permute-done.25 = bf16[512,256]{1,0:T(8,128)(2,1)} collective-permute-done((bf16[512,256]{1,0:T(8,128)(2,1)}, bf16[512,256]{1,0:T(8,128)(2,1)}, u32[]{:S(2)}, u32[]{:S(2)}) %collective-permute-start.25) | collective-permute-done | bytes 262176 | tf_op jit(solution)/shard_map/ppermute | solution.py:347
  123.7 1.3 add_convert_fusion.1
  125.4 4.7 %collective-permute-done.17 = bf16[512,512]{1,0:T(8,128)(2,1)S(1)} collective-permute-done((bf16[512,512]{1,0:T(8,128)(2,1)}, bf16[512,512]{1,0:T(8,128)(2,1)S(1)}, u32[]{:S(2)}, u32[]{:S(2)}) %collective-permute-start.17) | collective-permute-done | bytes 524320 | tf_op jit(solution)/shard_map/ppermute | solution.py:385
  130.0 7.1 %collective-permute-done.18 = bf16[512,512]{1,0:T(8,128)(2,1)S(1)} collective-permute-done((bf16[512,512]{1,0:T(8,128)(2,1)}, bf16[512,512]{1,0:T(8,128)(2,1)S(1)}, u32[]{:S(2)}, u32[]{:S(2)}) %collective-permute-start.18) | collective-permute-done | bytes 524320 | tf_op jit(solution)/shard_map/ppermute | solution.py:386
  137.2 1.1 maximum_bitcast_fusion
  138.3 6.4 %collective-permute-done.23 = bf16[512,256]{1,0:T(8,128)(2,1)S(1)} collective-permute-done((bf16[512,256]{1,0:T(8,128)(2,1)S(1)}, bf16[512,256]{1,0:T(8,128)(2,1)S(1)}, u32[]{:S(2)}, u32[]{:S(2)}) %collective-permute-start.23) | collective-permute-done | bytes 262176 | tf_op jit(solution)/shard_map/ppermute | solution.py:399
  144.7 5.7 %collective-permute-done.28 = bf16[512,256]{1,0:T(8,128)(2,1)S(1)} collective-permute-done((bf16[512,256]{1,0:T(8,128)(2,1)S(1)}, bf16[512,256]{1,0:T(8,128)(2,1)S(1)}, u32[]{:S(2)}, u32[]{:S(2)}) %collective-permute-start.28) | collective-permute-done | bytes 262176 | tf_op jit(solution)/shard_map/ppermute | solution.py:399
  150.5 0.7 slice_bitcast_fusion.8
  (43 shorter events, 3.5 us)
Async XLA Ops:
  1.6 9.6 %collective-permute-start.5 = (bf16[512,256]{1,0:T(8,128)(2,1)S(1)}, bf16[512,256]{1,0:T(8,128)(2,1)S(1)}, u32[]{:S(2)}, u32[]{:S(2)}) collective-permute-start(bf16[512,256]{1,0:T(8,128)(2,1)S(1)} %pad_maximum_fusion.refs_4_), channel_id=1, source_target_pairs={{0,8},{1,9},{2,10},{3,11},{4,12},{5,13},{6,14},{7,15},{8,0},{9,1},... | collective-permute-start | bytes 786440 | tf_op jit(solution)/shard_map/ppermute | solution.py:347
  4.9 6.4 %collective-permute-start.9 = (bf16[512,256]{1,0:T(8,128)(2,1)S(1)}, bf16[512,256]{1,0:T(8,128)(2,1)S(1)}, u32[]{:S(2)}, u32[]{:S(2)}) collective-permute-start(bf16[512,256]{1,0:T(8,128)(2,1)S(1)} %pad_maximum_fusion.refs_4_), channel_id=1, source_target_pairs={{0,1},{1,0},{2,3},{3,2},{4,5},{5,4},{6,7},{7,6},{8,9},{9,8},{10,11... | collective-permute-start | bytes 786440 | tf_op jit(solution)/shard_map/ppermute | solution.py:350
  4.9 15.9 %collective-permute-start.4 = (bf16[512,256]{1,0:T(8,128)(2,1)S(1)}, bf16[512,256]{1,0:T(8,128)(2,1)S(1)}, u32[]{:S(2)}, u32[]{:S(2)}) collective-permute-start(bf16[512,256]{1,0:T(8,128)(2,1)S(1)} %pad_maximum_fusion.refs_4_), channel_id=1, source_target_pairs={{0,6},{1,7},{2,0},{3,1},{4,2},{5,3},{6,4},{7,5},{8,14},{9,15},{10,... | collective-permute-start | bytes 786440 | tf_op jit(solution)/shard_map/ppermute | solution.py:347
  8.9 11.9 %collective-permute-start.3 = (bf16[512,256]{1,0:T(8,128)(2,1)S(1)}, bf16[512,256]{1,0:T(8,128)(2,1)S(1)}, u32[]{:S(2)}, u32[]{:S(2)}) collective-permute-start(bf16[512,256]{1,0:T(8,128)(2,1)S(1)} %pad_maximum_fusion.refs_4_), channel_id=1, source_target_pairs={{0,4},{1,5},{2,6},{3,7},{4,0},{5,1},{6,2},{7,3},{8,12},{9,13},{10,... | collective-permute-start | bytes 786440 | tf_op jit(solution)/shard_map/ppermute | solution.py:347
  8.9 15.6 %collective-permute-start.2 = (bf16[512,256]{1,0:T(8,128)(2,1)S(1)}, bf16[512,256]{1,0:T(8,128)(2,1)S(1)}, u32[]{:S(2)}, u32[]{:S(2)}) collective-permute-start(bf16[512,256]{1,0:T(8,128)(2,1)S(1)} %pad_maximum_fusion.refs_4_), channel_id=1, source_target_pairs={{0,2},{1,3},{2,4},{3,5},{4,6},{5,7},{6,0},{7,1},{8,10},{9,11},{10,... | collective-permute-start | bytes 786440 | tf_op jit(solution)/shard_map/ppermute | solution.py:347
  11.3 13.2 %collective-permute-start.13 = (bf16[512,256]{1,0:T(8,128)(2,1)S(1)}, bf16[512,256]{1,0:T(8,128)(2,1)S(1)}, u32[]{:S(2)}, u32[]{:S(2)}) collective-permute-start(bf16[512,256]{1,0:T(8,128)(2,1)S(1)} %collective-permute-done.5.refs_8_), channel_id=1, source_target_pairs={{0,1},{1,0},{2,3},{3,2},{4,5},{5,4},{6,7},{7,6},{8,9},{9,8},{10,11... | collective-permute-start | bytes 786440 | tf_op jit(solution)/shard_map/ppermute | solution.py:350
  11.3 34.0 %collective-permute-start = (bf16[512,1024]{1,0:T(8,128)(2,1)}, bf16[512,1024]{1,0:T(8,128)(2,1)}, u32[]{:S(2)}, u32[]{:S(2)}) collective-permute-start(bf16[512,1024]{1,0:T(8,128)(2,1)} %bitcast.53), channel_id=1, source_target_pairs={{0,1},{1,0},{2,3},{3,2},{4,5},{5,4},{6,7},{7,6},{8,9},{9,8},{10,11... | collective-permute-start | bytes 3145736 | tf_op jit(solution)/shard_map/ppermute | solution.py:350
  20.8 24.5 %collective-permute-start.1 = (bf16[512,1024]{1,0:T(8,128)(2,1)}, bf16[512,1024]{1,0:T(8,128)(2,1)}, u32[]{:S(2)}, u32[]{:S(2)}) collective-permute-start(bf16[512,1024]{1,0:T(8,128)(2,1)} %bitcast.55), channel_id=1, source_target_pairs={{0,1},{1,0},{2,3},{3,2},{4,5},{5,4},{6,7},{7,6},{8,9},{9,8},{10,11... | collective-permute-start | bytes 3145736 | tf_op jit(solution)/shard_map/ppermute | solution.py:350
  20.8 9.9 %collective-permute-start.8 = (bf16[512,256]{1,0:T(8,128)(2,1)S(1)}, bf16[512,256]{1,0:T(8,128)(2,1)S(1)}, u32[]{:S(2)}, u32[]{:S(2)}) collective-permute-start(bf16[512,256]{1,0:T(8,128)(2,1)S(1)} %collective-permute-done.5.refs_8_), channel_id=1, source_target_pairs={{0,6},{1,7},{2,0},{3,1},{4,2},{5,3},{6,4},{7,5},{8,14},{9,15},{10,... | collective-permute-start | bytes 786440 | tf_op jit(solution)/shard_map/ppermute | solution.py:347
  24.5 9.6 %collective-permute-start.6 = (bf16[512,256]{1,0:T(8,128)(2,1)S(1)}, bf16[512,256]{1,0:T(8,128)(2,1)S(1)}, u32[]{:S(2)}, u32[]{:S(2)}) collective-permute-start(bf16[512,256]{1,0:T(8,128)(2,1)S(1)} %collective-permute-done.5.refs_8_), channel_id=1, source_target_pairs={{0,2},{1,3},{2,4},{3,5},{4,6},{5,7},{6,0},{7,1},{8,10},{9,11},{10,... | collective-permute-start | bytes 786440 | tf_op jit(solution)/shard_map/ppermute | solution.py:347
  24.5 10.0 %collective-permute-start.12 = (bf16[512,256]{1,0:T(8,128)(2,1)S(1)}, bf16[512,256]{1,0:T(8,128)(2,1)S(1)}, u32[]{:S(2)}, u32[]{:S(2)}) collective-permute-start(bf16[512,256]{1,0:T(8,128)(2,1)S(1)} %collective-permute-done.4.refs_7_), channel_id=1, source_target_pairs={{0,1},{1,0},{2,3},{3,2},{4,5},{5,4},{6,7},{7,6},{8,9},{9,8},{10,11... | collective-permute-start | bytes 786440 | tf_op jit(solution)/shard_map/ppermute | solution.py:350
  30.7 3.8 %collective-permute-start.11 = (bf16[512,256]{1,0:T(8,128)(2,1)S(1)}, bf16[512,256]{1,0:T(8,128)(2,1)S(1)}, u32[]{:S(2)}, u32[]{:S(2)}) collective-permute-start(bf16[512,256]{1,0:T(8,128)(2,1)S(1)} %collective-permute-done.3.refs_6_), channel_id=1, source_target_pairs={{0,1},{1,0},{2,3},{3,2},{4,5},{5,4},{6,7},{7,6},{8,9},{9,8},{10,11... | collective-permute-start | bytes 786440 | tf_op jit(solution)/shard_map/ppermute | solution.py:350
  34.2 9.1 %collective-permute-start.7 = (bf16[512,256]{1,0:T(8,128)(2,1)S(1)}, bf16[512,256]{1,0:T(8,128)(2,1)S(1)}, u32[]{:S(2)}, u32[]{:S(2)}) collective-permute-start(bf16[512,256]{1,0:T(8,128)(2,1)S(1)} %collective-permute-done.3.refs_6_), channel_id=1, source_target_pairs={{0,8},{1,9},{2,10},{3,11},{4,12},{5,13},{6,14},{7,15},{8,0},{9,1},... | collective-permute-start | bytes 786440 | tf_op jit(solution)/shard_map/ppermute | solution.py:347
  34.5 8.8 %collective-permute-start.10 = (bf16[512,256]{1,0:T(8,128)(2,1)S(1)}, bf16[512,256]{1,0:T(8,128)(2,1)S(1)}, u32[]{:S(2)}, u32[]{:S(2)}) collective-permute-start(bf16[512,256]{1,0:T(8,128)(2,1)S(1)} %collective-permute-done.2.refs_5_), channel_id=1, source_target_pairs={{0,1},{1,0},{2,3},{3,2},{4,5},{5,4},{6,7},{7,6},{8,9},{9,8},{10,11... | collective-permute-start | bytes 786440 | tf_op jit(solution)/shard_map/ppermute | solution.py:350
  34.5 10.0 %collective-permute-start.16 = (bf16[512,256]{1,0:T(8,128)(2,1)S(1)}, bf16[512,256]{1,0:T(8,128)(2,1)}, u32[]{:S(2)}, u32[]{:S(2)}) collective-permute-start(bf16[512,256]{1,0:T(8,128)(2,1)S(1)} %collective-permute-done.8.refs_11_), channel_id=1, source_target_pairs={{0,1},{1,0},{2,3},{3,2},{4,5},{5,4},{6,7},{7,6},{8,9},{9,8},{10,11... | collective-permute-start | bytes 786440 | tf_op jit(solution)/shard_map/ppermute | solution.py:350
  43.2 1.7 %collective-permute-start.14 = (bf16[512,256]{1,0:T(8,128)(2,1)S(1)}, bf16[512,256]{1,0:T(8,128)(2,1)}, u32[]{:S(2)}, u32[]{:S(2)}) collective-permute-start(bf16[512,256]{1,0:T(8,128)(2,1)S(1)} %collective-permute-done.6.refs_9_), channel_id=1, source_target_pairs={{0,1},{1,0},{2,3},{3,2},{4,5},{5,4},{6,7},{7,6},{8,9},{9,8},{10,11... | collective-permute-start | bytes 786440 | tf_op jit(solution)/shard_map/ppermute | solution.py:350
  43.2 2.0 %collective-permute-start.15 = (bf16[512,256]{1,0:T(8,128)(2,1)S(1)}, bf16[512,256]{1,0:T(8,128)(2,1)}, u32[]{:S(2)}, u32[]{:S(2)}) collective-permute-start(bf16[512,256]{1,0:T(8,128)(2,1)S(1)} %collective-permute-done.7.refs_10_), channel_id=1, source_target_pairs={{0,1},{1,0},{2,3},{3,2},{4,5},{5,4},{6,7},{7,6},{8,9},{9,8},{10,11... | collective-permute-start | bytes 786440 | tf_op jit(solution)/shard_map/ppermute | solution.py:350
  93.6 3.4 %copy-start = (bf16[512,256]{1,0:T(8,128)(2,1)}, bf16[512,256]{1,0:T(8,128)(2,1)S(1)}, u32[]{:S(2)}) copy-start(bf16[512,256]{1,0:T(8,128)(2,1)S(1)} %get-tuple-element.30) | copy-start | bytes 786436
  93.7 3.1 %collective-permute-start.19 = (bf16[4,512,256]{2,1,0:T(8,128)(2,1)}, bf16[4,512,256]{2,1,0:T(8,128)(2,1)S(1)}, u32[]{:S(2)}, u32[]{:S(2)}) collective-permute-start(bf16[4,512,256]{2,1,0:T(8,128)(2,1)} %get-tuple-element.22), channel_id=1, source_target_pairs={{0,1},{1,0},{2,3},{3,2},{4,5},{5,4},{6,7},{7,6},{8,9},{9,8},{10,11... | collective-permute-start | bytes 3145736 | tf_op jit(solution)/shard_map/ppermute | solution.py:350
  94.0 6.3 %collective-permute-start.24 = (bf16[4,512,256]{2,1,0:T(8,128)(2,1)}, bf16[4,512,256]{2,1,0:T(8,128)(2,1)S(1)}, u32[]{:S(2)}, u32[]{:S(2)}) collective-permute-start(bf16[4,512,256]{2,1,0:T(8,128)(2,1)} %get-tuple-element.31), channel_id=1, source_target_pairs={{0,1},{1,0},{2,3},{3,2},{4,5},{5,4},{6,7},{7,6},{8,9},{9,8},{10,11... | collective-permute-start | bytes 3145736 | tf_op jit(solution)/shard_map/ppermute | solution.py:350
  97.0 15.8 %collective-permute-start.20 = (bf16[512,256]{1,0:T(8,128)(2,1)S(1)}, bf16[512,256]{1,0:T(8,128)(2,1)S(1)}, u32[]{:S(2)}, u32[]{:S(2)}) collective-permute-start(bf16[512,256]{1,0:T(8,128)(2,1)S(1)} %get-tuple-element.27), channel_id=1, source_target_pairs={{0,2},{1,3},{2,4},{3,5},{4,6},{5,7},{6,0},{7,1},{8,10},{9,11},{10,... | collective-permute-start | bytes 786440 | tf_op jit(solution)/shard_map/ppermute | solution.py:347
  97.1 15.8 %collective-permute-start.21 = (bf16[512,256]{1,0:T(8,128)(2,1)S(1)}, bf16[512,256]{1,0:T(8,128)(2,1)S(1)}, u32[]{:S(2)}, u32[]{:S(2)}) collective-permute-start(bf16[512,256]{1,0:T(8,128)(2,1)S(1)} %get-tuple-element.28), channel_id=1, source_target_pairs={{0,4},{1,5},{2,6},{3,7},{4,0},{5,1},{6,2},{7,3},{8,12},{9,13},{10,... | collective-permute-start | bytes 786440 | tf_op jit(solution)/shard_map/ppermute | solution.py:347
  97.2 16.8 %collective-permute-start.22 = (bf16[512,256]{1,0:T(8,128)(2,1)S(1)}, bf16[512,256]{1,0:T(8,128)(2,1)S(1)}, u32[]{:S(2)}, u32[]{:S(2)}) collective-permute-start(bf16[512,256]{1,0:T(8,128)(2,1)S(1)} %get-tuple-element.29), channel_id=1, source_target_pairs={{0,6},{1,7},{2,0},{3,1},{4,2},{5,3},{6,4},{7,5},{8,14},{9,15},{10,... | collective-permute-start | bytes 786440 | tf_op jit(solution)/shard_map/ppermute | solution.py:347
  101.3 22.3 %copy-start.1 = (bf16[512,256]{1,0:T(8,128)(2,1)S(1)}, bf16[512,256]{1,0:T(8,128)(2,1)}, u32[]{:S(2)}) copy-start(bf16[512,256]{1,0:T(8,128)(2,1)} %copy-done) | copy-start | bytes 786436
  101.4 22.3 %collective-permute-start.25 = (bf16[512,256]{1,0:T(8,128)(2,1)}, bf16[512,256]{1,0:T(8,128)(2,1)}, u32[]{:S(2)}, u32[]{:S(2)}) collective-permute-start(bf16[512,256]{1,0:T(8,128)(2,1)} %get-tuple-element.39), channel_id=1, source_target_pairs={{0,2},{1,3},{2,4},{3,5},{4,6},{5,7},{6,0},{7,1},{8,10},{9,11},{10,... | collective-permute-start | bytes 786440 | tf_op jit(solution)/shard_map/ppermute | solution.py:347
  102.2 21.4 %collective-permute-start.27 = (bf16[512,256]{1,0:T(8,128)(2,1)}, bf16[512,256]{1,0:T(8,128)(2,1)}, u32[]{:S(2)}, u32[]{:S(2)}) collective-permute-start(bf16[512,256]{1,0:T(8,128)(2,1)} %get-tuple-element.40), channel_id=1, source_target_pairs={{0,6},{1,7},{2,0},{3,1},{4,2},{5,3},{6,4},{7,5},{8,14},{9,15},{10,... | collective-permute-start | bytes 786440 | tf_op jit(solution)/shard_map/ppermute | solution.py:347
  112.9 10.7 %collective-permute-start.26 = (bf16[512,256]{1,0:T(8,128)(2,1)S(1)}, bf16[512,256]{1,0:T(8,128)(2,1)}, u32[]{:S(2)}, u32[]{:S(2)}) collective-permute-start(bf16[512,256]{1,0:T(8,128)(2,1)S(1)} %get-tuple-element.41), channel_id=1, source_target_pairs={{0,4},{1,5},{2,6},{3,7},{4,0},{5,1},{6,2},{7,3},{8,12},{9,13},{10,... | collective-permute-start | bytes 786440 | tf_op jit(solution)/shard_map/ppermute | solution.py:347
  112.9 17.1 %collective-permute-start.17 = (bf16[512,512]{1,0:T(8,128)(2,1)}, bf16[512,512]{1,0:T(8,128)(2,1)S(1)}, u32[]{:S(2)}, u32[]{:S(2)}) collective-permute-start(bf16[512,512]{1,0:T(8,128)(2,1)} %get-tuple-element.19), channel_id=1, source_target_pairs={{0,112},{1,113},{2,114},{3,115},{4,116},{5,117},{6,118},{7,119},{8... | collective-permute-start | bytes 1572872 | tf_op jit(solution)/shard_map/ppermute | solution.py:385
  114.0 0.7 copy-start.2
  114.7 22.4 %collective-permute-start.18 = (bf16[512,512]{1,0:T(8,128)(2,1)}, bf16[512,512]{1,0:T(8,128)(2,1)S(1)}, u32[]{:S(2)}, u32[]{:S(2)}) collective-permute-start(bf16[512,512]{1,0:T(8,128)(2,1)} %get-tuple-element.20), channel_id=1, source_target_pairs={{0,113},{1,112},{2,115},{3,114},{4,117},{5,116},{6,119},{7,118},{8... | collective-permute-start | bytes 1572872 | tf_op jit(solution)/shard_map/ppermute | solution.py:386
  123.6 21.1 %collective-permute-start.23 = (bf16[512,256]{1,0:T(8,128)(2,1)S(1)}, bf16[512,256]{1,0:T(8,128)(2,1)S(1)}, u32[]{:S(2)}, u32[]{:S(2)}) collective-permute-start(bf16[512,256]{1,0:T(8,128)(2,1)S(1)} %add_convert_fusion.2), channel_id=1, source_target_pairs={{0,120},{1,121},{2,122},{3,123},{4,124},{5,125},{6,126},{7,127},{8... | collective-permute-start | bytes 786440 | tf_op jit(solution)/shard_map/ppermute | solution.py:399
  124.9 25.5 %collective-permute-start.28 = (bf16[512,256]{1,0:T(8,128)(2,1)S(1)}, bf16[512,256]{1,0:T(8,128)(2,1)S(1)}, u32[]{:S(2)}, u32[]{:S(2)}) collective-permute-start(bf16[512,256]{1,0:T(8,128)(2,1)S(1)} %add_convert_fusion.1), channel_id=1, source_target_pairs={{0,112},{1,113},{2,114},{3,115},{4,116},{5,117},{6,118},{7,119},{8... | collective-permute-start | bytes 786440 | tf_op jit(solution)/shard_map/ppermute | solution.py:399

commit v4 on v3

--- a/solution.py
+++ b/solution.py
@@ -384,8 +384,11 @@
     far_swap, near_swap = swap(par_parts[1]), swap(par_parts[0])
     dq_same = lax.ppermute(dq_own, ("pipe", "ctx"), route(False))
     dq_flip = lax.ppermute(dq_par, ("pipe", "ctx"), route(True))
-    far = [total([own_parts[N_Z + i], far_swap[i]]).astype(jnp.bfloat16) for i in range(N_Z)]
+    ahead = total([own_parts[N_Z + 2], far_swap[2]]).astype(jnp.bfloat16)
+    ahead, far_swap = lax.optimization_barrier((ahead, far_swap))
+    far = [total([own_parts[N_Z + i], far_swap[i]]).astype(jnp.bfloat16) for i in (0, 1, 3)]
     far = lax.optimization_barrier(far)
+    far = [far[0], far[1], ahead, far[2]]
     far_in = [hop(far[dz], 0, dz) for dz in (1, 2, 3)]
     near = [total([own_parts[i], near_swap[i]]).astype(jnp.bfloat16) for i in range(N_Z)]
     near_in = [hop(near[dz], 0, dz) for dz in (1, 2, 3)]
@@ -400,11 +403,12 @@
 
     crossed = across(total([far[0]] + far_in).astype(jnp.bfloat16), 1)
     straight = across(total([near[0]] + near_in).astype(jnp.bfloat16), 0)
-    kv_out = total([crossed, straight]).astype(jnp.bfloat16)
+    k_out = total([crossed[:, :HD], straight[:, :HD]]).astype(jnp.bfloat16)
+    v_out = total([crossed[:, HD:], straight[:, HD:]]).astype(jnp.bfloat16)
     left = jnp.where(core == 0, dq_same, dq_flip)
     right = jnp.where(core == 0, dq_flip, dq_same)
     q_out = jnp.concatenate([left, right], axis=1)
-    return (q_out[None], kv_out[:, :HD][None], kv_out[:, HD:][None])
+    return (q_out[None], k_out[None], v_out[None])
 
 
 def solution(mesh):

time: 151 us -> 151 us (level)
  transfers between devices with their start and end apart: 29 -> 29, of which waited for: 15 -> 14; matrix products, arithmetic and copies ran while one was open for 4% -> 4% of each run, Pallas kernels for 0% -> 0%
where the time goes in v4:
time: 151 us
  waiting for transfers between devices  71.4 us (47%)
  Pallas kernels  48.4 us (32%)
  starting transfers between devices  22.5 us (15%)
  other arithmetic  7.27 us (5%)
    pallas_call x1, Pallas kernels, run_attention(): pl.pallas_call(functools.partial(attention_kernel, blocks=blocks, heads=h...  48.4 us
    ppermute x13, waiting for transfers between devices, hop(): return lax.ppermute(x, 'ctx', [(i, to(i)) for i in range(n_ctx)])  44.6 us
    ppermute x13, starting transfers between devices, hop(): return lax.ppermute(x, 'ctx', [(i, to(i)) for i in range(n_ctx)])  19.1 us
    ppermute x2, waiting for transfers between devices, across(): return lax.ppermute(x, ('pipe', 'ctx'), pairs)  11.7 us
    ppermute x1, waiting for transfers between devices, local(): dq_flip = lax.ppermute(dq_par, ('pipe', 'ctx'), route(True))  7.08 us
    ppermute x1, waiting for transfers between devices, local(): dq_same = lax.ppermute(dq_own, ('pipe', 'ctx'), route(False))  4.89 us
    ppermute x12, waiting for transfers between devices, swap(): return lax.ppermute(x, 'ctx', [(i, i ^ 1) for i in range(n_ctx)])  3.16 us
  transfers between devices with their start and end apart: 29, of which 14 were waited for; matrix products, arithmetic and copies ran while one was open for 4% of the time, Pallas kernels for 0%

profile of v4, /device:TPU:6, one launch (start us, length us, event | category | flops | bytes accessed | tf_op | source)
XLA Modules:
  0.0 151.0 jit_solution(13181617409804928021)
XLA Ops:
  0.6 1.0 pad_maximum_fusion.refs_4_
  1.6 3.3 %collective-permute-start.5 = (bf16[512,256]{1,0:T(8,128)(2,1)S(1)}, bf16[512,256]{1,0:T(8,128)(2,1)S(1)}, u32[]{:S(2)}, u32[]{:S(2)}) collective-permute-start(bf16[512,256]{1,0:T(8,128)(2,1)S(1)} %pad_maximum_fusion.refs_4_), channel_id=1, source_target_pairs={{0,8},{1,9},{2,10},{3,11},{4,12},{5,13},{6,14},{7,15},{8,0},{9,1},... | collective-permute-start | bytes 786440 | tf_op jit(solution)/shard_map/ppermute | solution.py:347
  4.9 4.0 %collective-permute-start.4 = (bf16[512,256]{1,0:T(8,128)(2,1)S(1)}, bf16[512,256]{1,0:T(8,128)(2,1)S(1)}, u32[]{:S(2)}, u32[]{:S(2)}) collective-permute-start(bf16[512,256]{1,0:T(8,128)(2,1)S(1)} %pad_maximum_fusion.refs_4_), channel_id=1, source_target_pairs={{0,6},{1,7},{2,0},{3,1},{4,2},{5,3},{6,4},{7,5},{8,14},{9,15},{10,... | collective-permute-start | bytes 786440 | tf_op jit(solution)/shard_map/ppermute | solution.py:347
  8.9 1.3 collective-permute-start.2
  10.2 1.1 collective-permute-done.5.refs_8_
  11.3 0.5 collective-permute-start
  11.8 9.0 %collective-permute-done.4.refs_7_ = bf16[512,256]{1,0:T(8,128)(2,1)S(1)} collective-permute-done((bf16[512,256]{1,0:T(8,128)(2,1)S(1)}, bf16[512,256]{1,0:T(8,128)(2,1)S(1)}, u32[]{:S(2)}, u32[]{:S(2)}) %collective-permute-start.4) | collective-permute-done | bytes 262176 | tf_op jit(solution)/shard_map/ppermute | solution.py:347
  20.8 3.7 %collective-permute-start.8 = (bf16[512,256]{1,0:T(8,128)(2,1)S(1)}, bf16[512,256]{1,0:T(8,128)(2,1)S(1)}, u32[]{:S(2)}, u32[]{:S(2)}) collective-permute-start(bf16[512,256]{1,0:T(8,128)(2,1)S(1)} %collective-permute-done.5.refs_8_), channel_id=1, source_target_pairs={{0,6},{1,7},{2,0},{3,1},{4,2},{5,3},{6,4},{7,5},{8,14},{9,15},{10,... | collective-permute-start | bytes 786440 | tf_op jit(solution)/shard_map/ppermute | solution.py:347
  24.8 5.9 %collective-permute-done.8.refs_11_ = bf16[512,256]{1,0:T(8,128)(2,1)S(1)} collective-permute-done((bf16[512,256]{1,0:T(8,128)(2,1)S(1)}, bf16[512,256]{1,0:T(8,128)(2,1)S(1)}, u32[]{:S(2)}, u32[]{:S(2)}) %collective-permute-start.8) | collective-permute-done | bytes 262176 | tf_op jit(solution)/shard_map/ppermute | solution.py:347
  30.7 3.4 %collective-permute-done.6.refs_9_ = bf16[512,256]{1,0:T(8,128)(2,1)S(1)} collective-permute-done((bf16[512,256]{1,0:T(8,128)(2,1)S(1)}, bf16[512,256]{1,0:T(8,128)(2,1)S(1)}, u32[]{:S(2)}, u32[]{:S(2)}) %collective-permute-start.6) | collective-permute-done | bytes 262176 | tf_op jit(solution)/shard_map/ppermute | solution.py:347
  34.5 0.5 collective-permute-start.16
  35.0 8.2 %collective-permute-done.7.refs_10_ = bf16[512,256]{1,0:T(8,128)(2,1)S(1)} collective-permute-done((bf16[512,256]{1,0:T(8,128)(2,1)S(1)}, bf16[512,256]{1,0:T(8,128)(2,1)S(1)}, u32[]{:S(2)}, u32[]{:S(2)}) %collective-permute-start.7) | collective-permute-done | bytes 262176 | tf_op jit(solution)/shard_map/ppermute | solution.py:347
  43.2 0.5 collective-permute-start.15
  43.8 0.7 pad_add_fusion.table
  45.3 48.4 %attention.1 = (bf16[512,256]{1,0:T(8,128)(2,1)S(1)}, bf16[512,256]{1,0:T(8,128)(2,1)S(1)}, bf16[512,256]{1,0:T(8,128)(2,1)S(1)}, bf16[512,256]{1,0:T(8,128)(2,1...) custom-call(s32[25]{0:T(128)S(1)} %pad_add_fusion.table, ...), custom_call_target="tpu_custom_call" | custom-call | tf_op jit(solution)/shard_map/attention/pallas_call | solution.py:308
  94.4 2.4 %collective-permute-done.19 = bf16[4,512,256]{2,1,0:T(8,128)(2,1)S(1)} collective-permute-done((bf16[4,512,256]{2,1,0:T(8,128)(2,1)}, bf16[4,512,256]{2,1,0:T(8,128)(2,1)S(1)}, u32[]{:S(2)}, u32[]{:S(2)}) %collective-permute-start.19) | collective-permute-done | bytes 1048608 | tf_op jit(solution)/shard_map/ppermute | solution.py:350
  97.1 3.2 %collective-permute-start.22 = (bf16[512,256]{1,0:T(8,128)(2,1)S(1)}, bf16[512,256]{1,0:T(8,128)(2,1)S(1)}, u32[]{:S(2)}, u32[]{:S(2)}) collective-permute-start(bf16[512,256]{1,0:T(8,128)(2,1)S(1)} %get-tuple-element.31), channel_id=1, source_target_pairs={{0,6},{1,7},{2,0},{3,1},{4,2},{5,3},{6,4},{7,5},{8,14},{9,15},{10,... | collective-permute-start | bytes 786440 | tf_op jit(solution)/shard_map/ppermute | solution.py:347
  100.4 1.0 fusion.2
  101.4 0.9 collective-permute-start.25
  102.2 2.4 %collective-permute-start.27 = (bf16[512,256]{1,0:T(8,128)(2,1)}, bf16[512,256]{1,0:T(8,128)(2,1)}, u32[]{:S(2)}, u32[]{:S(2)}) collective-permute-start(bf16[512,256]{1,0:T(8,128)(2,1)} %get-tuple-element.41), channel_id=1, source_target_pairs={{0,6},{1,7},{2,0},{3,1},{4,2},{5,3},{6,4},{7,5},{8,14},{9,15},{10,... | collective-permute-start | bytes 786440 | tf_op jit(solution)/shard_map/ppermute | solution.py:347
  104.6 8.5 %collective-permute-done.20 = bf16[512,256]{1,0:T(8,128)(2,1)S(1)} collective-permute-done((bf16[512,256]{1,0:T(8,128)(2,1)S(1)}, bf16[512,256]{1,0:T(8,128)(2,1)S(1)}, u32[]{:S(2)}, u32[]{:S(2)}) %collective-permute-start.20) | collective-permute-done | bytes 262176 | tf_op jit(solution)/shard_map/ppermute | solution.py:347
  113.5 0.7 copy-done.2
  114.2 1.1 add_convert_fusion.1
  115.3 8.4 %collective-permute-done.25 = bf16[512,256]{1,0:T(8,128)(2,1)} collective-permute-done((bf16[512,256]{1,0:T(8,128)(2,1)}, bf16[512,256]{1,0:T(8,128)(2,1)}, u32[]{:S(2)}, u32[]{:S(2)}) %collective-permute-start.25) | collective-permute-done | bytes 262176 | tf_op jit(solution)/shard_map/ppermute | solution.py:347
  123.7 1.3 add_convert_fusion
  124.9 0.4 collective-permute-start.28
  125.4 4.9 %collective-permute-done.17 = bf16[512,512]{1,0:T(8,128)(2,1)S(1)} collective-permute-done((bf16[512,512]{1,0:T(8,128)(2,1)}, bf16[512,512]{1,0:T(8,128)(2,1)S(1)}, u32[]{:S(2)}, u32[]{:S(2)}) %collective-permute-start.17) | collective-permute-done | bytes 524320 | tf_op jit(solution)/shard_map/ppermute | solution.py:385
  130.3 7.1 %collective-permute-done.18 = bf16[512,512]{1,0:T(8,128)(2,1)S(1)} collective-permute-done((bf16[512,512]{1,0:T(8,128)(2,1)}, bf16[512,512]{1,0:T(8,128)(2,1)S(1)}, u32[]{:S(2)}, u32[]{:S(2)}) %collective-permute-start.18) | collective-permute-done | bytes 524320 | tf_op jit(solution)/shard_map/ppermute | solution.py:386
  137.4 1.1 maximum_bitcast_fusion
  138.5 6.5 %collective-permute-done.23 = bf16[512,256]{1,0:T(8,128)(2,1)S(1)} collective-permute-done((bf16[512,256]{1,0:T(8,128)(2,1)S(1)}, bf16[512,256]{1,0:T(8,128)(2,1)S(1)}, u32[]{:S(2)}, u32[]{:S(2)}) %collective-permute-start.23) | collective-permute-done | bytes 262176 | tf_op jit(solution)/shard_map/ppermute | solution.py:402
  145.0 5.2 %collective-permute-done.28 = bf16[512,256]{1,0:T(8,128)(2,1)S(1)} collective-permute-done((bf16[512,256]{1,0:T(8,128)(2,1)S(1)}, bf16[512,256]{1,0:T(8,128)(2,1)S(1)}, u32[]{:S(2)}, u32[]{:S(2)}) %collective-permute-start.28) | collective-permute-done | bytes 262176 | tf_op jit(solution)/shard_map/ppermute | solution.py:402
  150.2 0.8 fusion.9
  (43 shorter events, 3.0 us)
Async XLA Ops:
  1.6 9.6 %collective-permute-start.5 = (bf16[512,256]{1,0:T(8,128)(2,1)S(1)}, bf16[512,256]{1,0:T(8,128)(2,1)S(1)}, u32[]{:S(2)}, u32[]{:S(2)}) collective-permute-start(bf16[512,256]{1,0:T(8,128)(2,1)S(1)} %pad_maximum_fusion.refs_4_), channel_id=1, source_target_pairs={{0,8},{1,9},{2,10},{3,11},{4,12},{5,13},{6,14},{7,15},{8,0},{9,1},... | collective-permute-start | bytes 786440 | tf_op jit(solution)/shard_map/ppermute | solution.py:347
  4.9 6.4 %collective-permute-start.9 = (bf16[512,256]{1,0:T(8,128)(2,1)S(1)}, bf16[512,256]{1,0:T(8,128)(2,1)S(1)}, u32[]{:S(2)}, u32[]{:S(2)}) collective-permute-start(bf16[512,256]{1,0:T(8,128)(2,1)S(1)} %pad_maximum_fusion.refs_4_), channel_id=1, source_target_pairs={{0,1},{1,0},{2,3},{3,2},{4,5},{5,4},{6,7},{7,6},{8,9},{9,8},{10,11... | collective-permute-start | bytes 786440 | tf_op jit(solution)/shard_map/ppermute | solution.py:350
  4.9 15.9 %collective-permute-start.4 = (bf16[512,256]{1,0:T(8,128)(2,1)S(1)}, bf16[512,256]{1,0:T(8,128)(2,1)S(1)}, u32[]{:S(2)}, u32[]{:S(2)}) collective-permute-start(bf16[512,256]{1,0:T(8,128)(2,1)S(1)} %pad_maximum_fusion.refs_4_), channel_id=1, source_target_pairs={{0,6},{1,7},{2,0},{3,1},{4,2},{5,3},{6,4},{7,5},{8,14},{9,15},{10,... | collective-permute-start | bytes 786440 | tf_op jit(solution)/shard_map/ppermute | solution.py:347
  8.9 11.9 %collective-permute-start.3 = (bf16[512,256]{1,0:T(8,128)(2,1)S(1)}, bf16[512,256]{1,0:T(8,128)(2,1)S(1)}, u32[]{:S(2)}, u32[]{:S(2)}) collective-permute-start(bf16[512,256]{1,0:T(8,128)(2,1)S(1)} %pad_maximum_fusion.refs_4_), channel_id=1, source_target_pairs={{0,4},{1,5},{2,6},{3,7},{4,0},{5,1},{6,2},{7,3},{8,12},{9,13},{10,... | collective-permute-start | bytes 786440 | tf_op jit(solution)/shard_map/ppermute | solution.py:347
  8.9 15.6 %collective-permute-start.2 = (bf16[512,256]{1,0:T(8,128)(2,1)S(1)}, bf16[512,256]{1,0:T(8,128)(2,1)S(1)}, u32[]{:S(2)}, u32[]{:S(2)}) collective-permute-start(bf16[512,256]{1,0:T(8,128)(2,1)S(1)} %pad_maximum_fusion.refs_4_), channel_id=1, source_target_pairs={{0,2},{1,3},{2,4},{3,5},{4,6},{5,7},{6,0},{7,1},{8,10},{9,11},{10,... | collective-permute-start | bytes 786440 | tf_op jit(solution)/shard_map/ppermute | solution.py:347
  11.3 13.2 %collective-permute-start.13 = (bf16[512,256]{1,0:T(8,128)(2,1)S(1)}, bf16[512,256]{1,0:T(8,128)(2,1)S(1)}, u32[]{:S(2)}, u32[]{:S(2)}) collective-permute-start(bf16[512,256]{1,0:T(8,128)(2,1)S(1)} %collective-permute-done.5.refs_8_), channel_id=1, source_target_pairs={{0,1},{1,0},{2,3},{3,2},{4,5},{5,4},{6,7},{7,6},{8,9},{9,8},{10,11... | collective-permute-start | bytes 786440 | tf_op jit(solution)/shard_map/ppermute | solution.py:350
  11.3 34.0 %collective-permute-start = (bf16[512,1024]{1,0:T(8,128)(2,1)}, bf16[512,1024]{1,0:T(8,128)(2,1)}, u32[]{:S(2)}, u32[]{:S(2)}) collective-permute-start(bf16[512,1024]{1,0:T(8,128)(2,1)} %bitcast.47), channel_id=1, source_target_pairs={{0,1},{1,0},{2,3},{3,2},{4,5},{5,4},{6,7},{7,6},{8,9},{9,8},{10,11... | collective-permute-start | bytes 3145736 | tf_op jit(solution)/shard_map/ppermute | solution.py:350
  20.8 24.5 %collective-permute-start.1 = (bf16[512,1024]{1,0:T(8,128)(2,1)}, bf16[512,1024]{1,0:T(8,128)(2,1)}, u32[]{:S(2)}, u32[]{:S(2)}) collective-permute-start(bf16[512,1024]{1,0:T(8,128)(2,1)} %bitcast.49), channel_id=1, source_target_pairs={{0,1},{1,0},{2,3},{3,2},{4,5},{5,4},{6,7},{7,6},{8,9},{9,8},{10,11... | collective-permute-start | bytes 3145736 | tf_op jit(solution)/shard_map/ppermute | solution.py:350
  20.8 9.9 %collective-permute-start.8 = (bf16[512,256]{1,0:T(8,128)(2,1)S(1)}, bf16[512,256]{1,0:T(8,128)(2,1)S(1)}, u32[]{:S(2)}, u32[]{:S(2)}) collective-permute-start(bf16[512,256]{1,0:T(8,128)(2,1)S(1)} %collective-permute-done.5.refs_8_), channel_id=1, source_target_pairs={{0,6},{1,7},{2,0},{3,1},{4,2},{5,3},{6,4},{7,5},{8,14},{9,15},{10,... | collective-permute-start | bytes 786440 | tf_op jit(solution)/shard_map/ppermute | solution.py:347
  24.5 9.6 %collective-permute-start.6 = (bf16[512,256]{1,0:T(8,128)(2,1)S(1)}, bf16[512,256]{1,0:T(8,128)(2,1)S(1)}, u32[]{:S(2)}, u32[]{:S(2)}) collective-permute-start(bf16[512,256]{1,0:T(8,128)(2,1)S(1)} %collective-permute-done.5.refs_8_), channel_id=1, source_target_pairs={{0,2},{1,3},{2,4},{3,5},{4,6},{5,7},{6,0},{7,1},{8,10},{9,11},{10,... | collective-permute-start | bytes 786440 | tf_op jit(solution)/shard_map/ppermute | solution.py:347
  24.5 10.0 %collective-permute-start.12 = (bf16[512,256]{1,0:T(8,128)(2,1)S(1)}, bf16[512,256]{1,0:T(8,128)(2,1)S(1)}, u32[]{:S(2)}, u32[]{:S(2)}) collective-permute-start(bf16[512,256]{1,0:T(8,128)(2,1)S(1)} %collective-permute-done.4.refs_7_), channel_id=1, source_target_pairs={{0,1},{1,0},{2,3},{3,2},{4,5},{5,4},{6,7},{7,6},{8,9},{9,8},{10,11... | collective-permute-start | bytes 786440 | tf_op jit(solution)/shard_map/ppermute | solution.py:350
  30.7 3.8 %collective-permute-start.11 = (bf16[512,256]{1,0:T(8,128)(2,1)S(1)}, bf16[512,256]{1,0:T(8,128)(2,1)S(1)}, u32[]{:S(2)}, u32[]{:S(2)}) collective-permute-start(bf16[512,256]{1,0:T(8,128)(2,1)S(1)} %collective-permute-done.3.refs_6_), channel_id=1, source_target_pairs={{0,1},{1,0},{2,3},{3,2},{4,5},{5,4},{6,7},{7,6},{8,9},{9,8},{10,11... | collective-permute-start | bytes 786440 | tf_op jit(solution)/shard_map/ppermute | solution.py:350
  34.2 9.1 %collective-permute-start.7 = (bf16[512,256]{1,0:T(8,128)(2,1)S(1)}, bf16[512,256]{1,0:T(8,128)(2,1)S(1)}, u32[]{:S(2)}, u32[]{:S(2)}) collective-permute-start(bf16[512,256]{1,0:T(8,128)(2,1)S(1)} %collective-permute-done.3.refs_6_), channel_id=1, source_target_pairs={{0,8},{1,9},{2,10},{3,11},{4,12},{5,13},{6,14},{7,15},{8,0},{9,1},... | collective-permute-start | bytes 786440 | tf_op jit(solution)/shard_map/ppermute | solution.py:347
  34.5 8.8 %collective-permute-start.10 = (bf16[512,256]{1,0:T(8,128)(2,1)S(1)}, bf16[512,256]{1,0:T(8,128)(2,1)S(1)}, u32[]{:S(2)}, u32[]{:S(2)}) collective-permute-start(bf16[512,256]{1,0:T(8,128)(2,1)S(1)} %collective-permute-done.2.refs_5_), channel_id=1, source_target_pairs={{0,1},{1,0},{2,3},{3,2},{4,5},{5,4},{6,7},{7,6},{8,9},{9,8},{10,11... | collective-permute-start | bytes 786440 | tf_op jit(solution)/shard_map/ppermute | solution.py:350
  34.5 10.0 %collective-permute-start.16 = (bf16[512,256]{1,0:T(8,128)(2,1)S(1)}, bf16[512,256]{1,0:T(8,128)(2,1)}, u32[]{:S(2)}, u32[]{:S(2)}) collective-permute-start(bf16[512,256]{1,0:T(8,128)(2,1)S(1)} %collective-permute-done.8.refs_11_), channel_id=1, source_target_pairs={{0,1},{1,0},{2,3},{3,2},{4,5},{5,4},{6,7},{7,6},{8,9},{9,8},{10,11... | collective-permute-start | bytes 786440 | tf_op jit(solution)/shard_map/ppermute | solution.py:350
  43.2 1.7 %collective-permute-start.14 = (bf16[512,256]{1,0:T(8,128)(2,1)S(1)}, bf16[512,256]{1,0:T(8,128)(2,1)}, u32[]{:S(2)}, u32[]{:S(2)}) collective-permute-start(bf16[512,256]{1,0:T(8,128)(2,1)S(1)} %collective-permute-done.6.refs_9_), channel_id=1, source_target_pairs={{0,1},{1,0},{2,3},{3,2},{4,5},{5,4},{6,7},{7,6},{8,9},{9,8},{10,11... | collective-permute-start | bytes 786440 | tf_op jit(solution)/shard_map/ppermute | solution.py:350
  43.2 2.0 %collective-permute-start.15 = (bf16[512,256]{1,0:T(8,128)(2,1)S(1)}, bf16[512,256]{1,0:T(8,128)(2,1)}, u32[]{:S(2)}, u32[]{:S(2)}) collective-permute-start(bf16[512,256]{1,0:T(8,128)(2,1)S(1)} %collective-permute-done.7.refs_10_), channel_id=1, source_target_pairs={{0,1},{1,0},{2,3},{3,2},{4,5},{5,4},{6,7},{7,6},{8,9},{9,8},{10,11... | collective-permute-start | bytes 786440 | tf_op jit(solution)/shard_map/ppermute | solution.py:350
  93.6 3.4 %copy-start = (bf16[512,256]{1,0:T(8,128)(2,1)}, bf16[512,256]{1,0:T(8,128)(2,1)S(1)}, u32[]{:S(2)}) copy-start(bf16[512,256]{1,0:T(8,128)(2,1)S(1)} %get-tuple-element.32) | copy-start | bytes 786436
  93.7 3.1 %collective-permute-start.19 = (bf16[4,512,256]{2,1,0:T(8,128)(2,1)}, bf16[4,512,256]{2,1,0:T(8,128)(2,1)S(1)}, u32[]{:S(2)}, u32[]{:S(2)}) collective-permute-start(bf16[4,512,256]{2,1,0:T(8,128)(2,1)} %get-tuple-element.24), channel_id=1, source_target_pairs={{0,1},{1,0},{2,3},{3,2},{4,5},{5,4},{6,7},{7,6},{8,9},{9,8},{10,11... | collective-permute-start | bytes 3145736 | tf_op jit(solution)/shard_map/ppermute | solution.py:350
  94.0 6.3 %collective-permute-start.24 = (bf16[4,512,256]{2,1,0:T(8,128)(2,1)}, bf16[4,512,256]{2,1,0:T(8,128)(2,1)S(1)}, u32[]{:S(2)}, u32[]{:S(2)}) collective-permute-start(bf16[4,512,256]{2,1,0:T(8,128)(2,1)} %get-tuple-element.33), channel_id=1, source_target_pairs={{0,1},{1,0},{2,3},{3,2},{4,5},{5,4},{6,7},{7,6},{8,9},{9,8},{10,11... | collective-permute-start | bytes 3145736 | tf_op jit(solution)/shard_map/ppermute | solution.py:350
  97.1 16.1 %collective-permute-start.20 = (bf16[512,256]{1,0:T(8,128)(2,1)S(1)}, bf16[512,256]{1,0:T(8,128)(2,1)S(1)}, u32[]{:S(2)}, u32[]{:S(2)}) collective-permute-start(bf16[512,256]{1,0:T(8,128)(2,1)S(1)} %get-tuple-element.29), channel_id=1, source_target_pairs={{0,2},{1,3},{2,4},{3,5},{4,6},{5,7},{6,0},{7,1},{8,10},{9,11},{10,... | collective-permute-start | bytes 786440 | tf_op jit(solution)/shard_map/ppermute | solution.py:347
  97.1 16.0 %collective-permute-start.22 = (bf16[512,256]{1,0:T(8,128)(2,1)S(1)}, bf16[512,256]{1,0:T(8,128)(2,1)S(1)}, u32[]{:S(2)}, u32[]{:S(2)}) collective-permute-start(bf16[512,256]{1,0:T(8,128)(2,1)S(1)} %get-tuple-element.31), channel_id=1, source_target_pairs={{0,6},{1,7},{2,0},{3,1},{4,2},{5,3},{6,4},{7,5},{8,14},{9,15},{10,... | collective-permute-start | bytes 786440 | tf_op jit(solution)/shard_map/ppermute | solution.py:347
  100.4 13.1 %collective-permute-start.21 = (bf16[512,256]{1,0:T(8,128)(2,1)S(1)}, bf16[512,256]{1,0:T(8,128)(2,1)S(1)}, u32[]{:S(2)}, u32[]{:S(2)}) collective-permute-start(bf16[512,256]{1,0:T(8,128)(2,1)S(1)} %fusion.7), channel_id=1, source_target_pairs={{0,4},{1,5},{2,6},{3,7},{4,0},{5,1},{6,2},{7,3},{8,12},{9,13},{10,... | collective-permute-start | bytes 786440 | tf_op jit(solution)/shard_map/ppermute | solution.py:347
  101.4 22.3 %copy-start.1 = (bf16[512,256]{1,0:T(8,128)(2,1)S(1)}, bf16[512,256]{1,0:T(8,128)(2,1)}, u32[]{:S(2)}) copy-start(bf16[512,256]{1,0:T(8,128)(2,1)} %copy-done) | copy-start | bytes 786436
  101.4 22.3 %collective-permute-start.25 = (bf16[512,256]{1,0:T(8,128)(2,1)}, bf16[512,256]{1,0:T(8,128)(2,1)}, u32[]{:S(2)}, u32[]{:S(2)}) collective-permute-start(bf16[512,256]{1,0:T(8,128)(2,1)} %get-tuple-element.40), channel_id=1, source_target_pairs={{0,2},{1,3},{2,4},{3,5},{4,6},{5,7},{6,0},{7,1},{8,10},{9,11},{10,... | collective-permute-start | bytes 786440 | tf_op jit(solution)/shard_map/ppermute | solution.py:347
  102.2 21.4 %collective-permute-start.27 = (bf16[512,256]{1,0:T(8,128)(2,1)}, bf16[512,256]{1,0:T(8,128)(2,1)}, u32[]{:S(2)}, u32[]{:S(2)}) collective-permute-start(bf16[512,256]{1,0:T(8,128)(2,1)} %get-tuple-element.41), channel_id=1, source_target_pairs={{0,6},{1,7},{2,0},{3,1},{4,2},{5,3},{6,4},{7,5},{8,14},{9,15},{10,... | collective-permute-start | bytes 786440 | tf_op jit(solution)/shard_map/ppermute | solution.py:347
  113.1 10.5 %collective-permute-start.26 = (bf16[512,256]{1,0:T(8,128)(2,1)S(1)}, bf16[512,256]{1,0:T(8,128)(2,1)}, u32[]{:S(2)}, u32[]{:S(2)}) collective-permute-start(bf16[512,256]{1,0:T(8,128)(2,1)S(1)} %get-tuple-element.42), channel_id=1, source_target_pairs={{0,4},{1,5},{2,6},{3,7},{4,0},{5,1},{6,2},{7,3},{8,12},{9,13},{10,... | collective-permute-start | bytes 786440 | tf_op jit(solution)/shard_map/ppermute | solution.py:347
  113.1 17.1 %collective-permute-start.17 = (bf16[512,512]{1,0:T(8,128)(2,1)}, bf16[512,512]{1,0:T(8,128)(2,1)S(1)}, u32[]{:S(2)}, u32[]{:S(2)}) collective-permute-start(bf16[512,512]{1,0:T(8,128)(2,1)} %get-tuple-element.20), channel_id=1, source_target_pairs={{0,112},{1,113},{2,114},{3,115},{4,116},{5,117},{6,118},{7,119},{8... | collective-permute-start | bytes 1572872 | tf_op jit(solution)/shard_map/ppermute | solution.py:385
  113.5 0.7 copy-start.2
  114.2 23.2 %collective-permute-start.18 = (bf16[512,512]{1,0:T(8,128)(2,1)}, bf16[512,512]{1,0:T(8,128)(2,1)S(1)}, u32[]{:S(2)}, u32[]{:S(2)}) collective-permute-start(bf16[512,512]{1,0:T(8,128)(2,1)} %get-tuple-element.21), channel_id=1, source_target_pairs={{0,113},{1,112},{2,115},{3,114},{4,117},{5,116},{6,119},{7,118},{8... | collective-permute-start | bytes 1572872 | tf_op jit(solution)/shard_map/ppermute | solution.py:386
  123.6 21.4 %collective-permute-start.23 = (bf16[512,256]{1,0:T(8,128)(2,1)S(1)}, bf16[512,256]{1,0:T(8,128)(2,1)S(1)}, u32[]{:S(2)}, u32[]{:S(2)}) collective-permute-start(bf16[512,256]{1,0:T(8,128)(2,1)S(1)} %add_convert_fusion.1), channel_id=1, source_target_pairs={{0,120},{1,121},{2,122},{3,123},{4,124},{5,125},{6,126},{7,127},{8... | collective-permute-start | bytes 786440 | tf_op jit(solution)/shard_map/ppermute | solution.py:402
  124.9 25.3 %collective-permute-start.28 = (bf16[512,256]{1,0:T(8,128)(2,1)S(1)}, bf16[512,256]{1,0:T(8,128)(2,1)S(1)}, u32[]{:S(2)}, u32[]{:S(2)}) collective-permute-start(bf16[512,256]{1,0:T(8,128)(2,1)S(1)} %add_convert_fusion), channel_id=1, source_target_pairs={{0,112},{1,113},{2,114},{3,115},{4,116},{5,117},{6,118},{7,119},{8... | collective-permute-start | bytes 786440 | tf_op jit(solution)/shard_map/ppermute | solution.py:402
